TPU v7x, 256 devices: a whole 4x4x8 slice. The times are simulated.
256 devices in a mesh: sec: 8 (over z_lo, core), ctx: 32 (over z_hi, x, y).
Axes of the slice: x: 4, y: 4, z: 8 (z_hi: 2, z_lo: 4; z = z_hi * 4 + z_lo), core: 2. Of those that a mesh axis runs over, the one named last changes fastest.
Arguments:
- q_frames: bfloat16 [8, 512, 8, 3584], P('sec', 'ctx'), may hold values from -8 to 8
- k_frames: bfloat16 [8, 512, 8, 512], P('sec', 'ctx'), may hold values from -8 to 8
- v_frames: bfloat16 [8, 512, 8, 512], P('sec', 'ctx'), may hold values from -6 to 6
- video_frames: int32 [8], replicated, may hold values from 256 to 512, as said below
- frame_section: int32 [8, 512], P('sec', 'ctx'), may hold values from 0 to 7, as said below
- frame_offset: int32 [8, 512], P('sec', 'ctx'), may hold values from 0 to 4088, as said below
Outputs:
- attention_out: bfloat16 [8, 4096, 3584], P('sec', 'ctx')
Inputs may be any that keep to these rules, and one draw needn't show every extreme that they name: `video_frames`: at least one section's video fills all 512 slots. `frame_section`: every device holds exactly 2 frame slots for each section. `frame_offset`: A multiple of 8; it falls in the 128 positions of the section's device whose ctx index equals that of the slot's device; the slots of one section cover its positions once. Slots at positions of frames beyond the video's length are not part of it.
All inputs are finite; a program needn't handle non-finite values.
Results may differ from a plain program's by a relative error of at most 0.006.
Values may be sent and summed in bfloat16 or wider, within the bound.
No kernel may reach another device: no remote copies, remote signals or barrier semaphores. Data moves between devices by JAX's collectives and lax.ppermute only.
A program may use at most 128 MiB of HBM per device.

v0:
```python
import math

import jax
import jax.numpy as jnp
from jax import lax
from jax.sharding import PartitionSpec as P

HEAD_DIM = 128


floor_score = -1e30


def source_slots(target_slot):
    slot_count = target_slot.shape[0]
    slot_ids = jnp.arange(slot_count, dtype=jnp.int32)
    matches = (target_slot[:, None] == slot_ids[None, :]).astype(jnp.int32)
    return jnp.sum(slot_ids[:, None] * matches, axis=0)


def make_absorb(query_sets, live_len, kv_heads, head_dim, score_scale):

    def absorb(carry, kv_piece, piece_start):
        key_block, value_block = kv_piece
        key_count = key_block.shape[0]
        key_pos = jnp.arange(key_count, dtype=jnp.int32)
        key_rows = key_block.reshape(key_count, kv_heads, head_dim)
        value_rows = value_block.reshape(key_count, kv_heads, head_dim)
        result = []
        for (queries, first_pos), carry_state in zip(query_sets, carry):
            row_count = queries.shape[0]
            active = (
                (piece_start <= first_pos + row_count - 1)
                & (piece_start < live_len)
                & (first_pos < live_len)
            )

            def advance(old_state, queries=queries, first_pos=first_pos, row_count=row_count):
                run_max, weight_sum, accumulated = old_state
                query_pos = first_pos + jnp.arange(row_count, dtype=jnp.int32)
                scores = (
                    jnp.einsum(
                        "rkgd,nkd->kgrn", queries, key_rows, preferred_element_type=jnp.float32
                    )
                    * score_scale
                )
                visible = (key_pos[None, :] <= query_pos[:, None]) & (key_pos[None, :] < live_len)
                masked = jnp.where(visible, scores, floor_score)
                new_max = jnp.maximum(run_max, jnp.max(masked, axis=-1))
                weights = jnp.where(visible, jnp.exp(scores - new_max[..., None]), 0.0)
                weight_sum = jnp.sum(weights, axis=-1)
                mixed = jnp.einsum(
                    "kgrn,nkd->rkgd",
                    weights.astype(jnp.bfloat16),
                    value_rows,
                    preferred_element_type=jnp.float32,
                )
                accumulated = mixed
                return (new_max, weight_sum, accumulated)

            result.append(lax.cond(active, advance, lambda unchanged: unchanged, carry_state))
        return tuple(result)

    return absorb


def finish(carry_state, first_pos, row_count, live_len):
    run_max, weight_sum, accumulated = carry_state
    query_pos = first_pos + jnp.arange(row_count, dtype=jnp.int32)
    is_live = query_pos < live_len
    safe_sum = jnp.where(is_live[None, None, :], weight_sum, 1.0)
    mixed = accumulated / jnp.transpose(safe_sum, (2, 0, 1))[..., None]
    mixed = mixed.reshape(row_count, -1)
    return jnp.where(is_live[:, None], mixed, 0.0).astype(jnp.bfloat16)


def local(q_frames, k_frames, v_frames, video_frames, frame_section, frame_offset):
    sections = lax.axis_size("sec")
    frames_dev = q_frames.shape[1]
    frame_len = q_frames.shape[2]
    per_section = frames_dev // sections
    kv_width = k_frames.shape[3]
    q_width = q_frames.shape[3]
    head_dim = HEAD_DIM
    kv_heads = kv_width // head_dim
    group_size = q_width // kv_width
    my_section = lax.axis_index("sec")
    my_place = lax.axis_index("ctx")
    section_of = frame_section[0]
    offsets = frame_offset[0]
    slot_ids = jnp.arange(frames_dev, dtype=jnp.int32)
    earlier = (section_of[:, None] == section_of[None, :]) & (slot_ids[None, :] < slot_ids[:, None])
    rank_in = jnp.sum(earlier.astype(jnp.int32), axis=1)
    order = source_slots(section_of * per_section + rank_in)
    send_q = jnp.take(q_frames[0], order, axis=0).reshape(sections, per_section, frame_len, q_width)
    send_k = jnp.take(k_frames[0], order, axis=0).reshape(
        sections, per_section, frame_len, kv_width
    )
    send_v = jnp.take(v_frames[0], order, axis=0).reshape(
        sections, per_section, frame_len, kv_width
    )
    send_off = jnp.take(offsets, order, axis=0).reshape(sections, per_section)
    got_q, got_k, got_v, got_off = (
        lax.all_to_all(send_q, "sec", split_axis=0, concat_axis=0, tiled=True),
        lax.all_to_all(send_k, "sec", split_axis=0, concat_axis=0, tiled=True),
        lax.all_to_all(send_v, "sec", split_axis=0, concat_axis=0, tiled=True),
        lax.all_to_all(send_off, "sec", split_axis=0, concat_axis=0, tiled=True),
    )
    local_slot = got_off.reshape(frames_dev) // frame_len - my_place * frames_dev
    placing = source_slots(local_slot)
    row_count = frames_dev * frame_len
    local_q = jnp.take(got_q.reshape(frames_dev, frame_len, q_width), placing, axis=0).reshape(
        row_count, q_width
    )
    local_k = jnp.take(got_k.reshape(frames_dev, frame_len, kv_width), placing, axis=0).reshape(
        row_count, kv_width
    )
    local_v = jnp.take(got_v.reshape(frames_dev, frame_len, kv_width), placing, axis=0).reshape(
        row_count, kv_width
    )
    live_len = video_frames[my_section] * frame_len
    half_rows = row_count // 2
    base_pos = my_place * row_count
    lead_q = local_q[:half_rows]
    tail_q = local_q[half_rows:]
    first_set = (lead_q, base_pos)
    second_set = (tail_q, base_pos + half_rows)
    query_sets = []
    for queries, first_pos in (first_set, second_set):
        query_sets.append((queries.reshape(half_rows, kv_heads, group_size, head_dim), first_pos))
    empty_state = (
        jnp.full((kv_heads, group_size, half_rows), floor_score, jnp.float32),
        jnp.zeros((kv_heads, group_size, half_rows), jnp.float32),
        jnp.zeros((half_rows, kv_heads, group_size, head_dim), jnp.float32),
    )
    absorb = make_absorb(query_sets, live_len, kv_heads, head_dim, 1.0 / math.sqrt(head_dim))
    states = absorb(
        (empty_state, empty_state),
        (
            lax.all_gather(local_k, "ctx", axis=0, tiled=True),
            lax.all_gather(local_v, "ctx", axis=0, tiled=True),
        ),
        jnp.int32(0),
    )
    first_out = finish(states[0], first_set[1], half_rows, live_len)
    second_out = finish(states[1], second_set[1], half_rows, live_len)
    return jnp.concatenate([first_out, second_out], axis=0)[None]


def solution(mesh):
    placed = (
        P("sec", "ctx", None, None),
        P("sec", "ctx", None, None),
        P("sec", "ctx", None, None),
        P(),
        P("sec", "ctx"),
        P("sec", "ctx"),
    )
    return jax.shard_map(
        local, mesh=mesh, in_specs=placed, out_specs=P("sec", "ctx", None), check_vma=False
    )
```

profile of v0, /device:TPU:32, one launch (start us, length us, event | category | flops | bytes accessed | tf_op | source)
XLA Modules:
  0.0 373.2 jit_solution(9911036601801687669)
XLA Ops:
  6.5 0.9 convert_reduce_fusion
  7.5 0.7 multiply_add_fusion
  8.1 0.1 select_reduce_fusion.1
  8.2 0.1 reduce_sum.51
  8.3 1.3 gather_fusion
  9.6 0.1 gather.13
  9.7 0.6 and_select_fusion
  10.3 6.0 %all-to-all-start.1 = ((s32[8,1,2]{2,1,0:T(1,128)}), s32[8,1,2]{2,1,0:T(1,128)S(1)}, u32[]{:S(2)}, u32[]{:S(2)}) async-start(s32[8,1,2]{2,1,0:T(1,128)} %bitcast.13), calls=%async_computation.1 | async-start | bytes 8192 | tf_op jit(solution)/shard_map/all_to_all | solution.py:107
  16.4 1.5 gather_fusion.5
  17.8 1.5 gather_fusion.3
  19.3 0.8 broadcast_select_fusion.2
  20.1 0.3 all-to-all-done.1
  20.4 4.8 %all-to-all-start.2 = ((bf16[8,2,8,512]{3,2,1,0:T(8,128)(2,1)}), bf16[8,2,8,512]{3,2,1,0:T(8,128)(2,1)S(1)}, u32[]{:S(2)}, u32[]{:S(2)}) async-start(bf16[8,2,8,512]{3,2,1,0:T(8,128)(2,1)} %bitcast.18), calls=%async_computation.2 | async-start | bytes 262144 | tf_op jit(solution)/shard_map/all_to_all | solution.py:105
  25.2 0.6 broadcast.297
  25.8 0.6 reduce.3
  26.4 0.1 reshape.217
  26.5 0.1 select_reduce_fusion
  26.6 4.3 %all-to-all-done.2 = bf16[8,2,8,512]{3,2,1,0:T(8,128)(2,1)S(1)} async-done(((bf16[8,2,8,512]{3,2,1,0:T(8,128)(2,1)}), bf16[8,2,8,512]{3,2,1,0:T(8,128)(2,1)S(1)}, u32[]{:S(2)}, u32[]{:S(2)}) %all-to-all-start.2) | async-done | bytes 131104 | tf_op jit(solution)/shard_map/all_to_all | solution.py:105
  30.9 4.4 %all-to-all-start.3 = ((bf16[8,2,8,512]{3,2,1,0:T(8,128)(2,1)}), bf16[8,2,8,512]{3,2,1,0:T(8,128)(2,1)S(1)}, u32[]{:S(2)}, u32[]{:S(2)}) async-start(bf16[8,2,8,512]{3,2,1,0:T(8,128)(2,1)} %bitcast.23), calls=%async_computation.3 | async-start | bytes 262144 | tf_op jit(solution)/shard_map/all_to_all | solution.py:106
  35.3 0.0 all-gather.5.cloned.1.call-start
  35.3 0.6 gather_fusion.4
  35.8 5.1 %all-to-all-done.3 = bf16[8,2,8,512]{3,2,1,0:T(8,128)(2,1)S(1)} async-done(((bf16[8,2,8,512]{3,2,1,0:T(8,128)(2,1)}), bf16[8,2,8,512]{3,2,1,0:T(8,128)(2,1)S(1)}, u32[]{:S(2)}, u32[]{:S(2)}) %all-to-all-start.3) | async-done | bytes 131104 | tf_op jit(solution)/shard_map/all_to_all | solution.py:106
  41.0 0.6 gather_fusion.6
  41.5 0.8 select_bitcast_fusion
  42.3 0.0 all-gather.5.cloned.1.call-update
  42.4 0.0 all-gather.3.cloned.1.call-start
  42.4 0.7 all-gather.3.cloned.1.call-update
  43.1 0.6 gather_fusion.1
  43.7 1.1 broadcast_select_fusion.1
  44.8 4.6 %all-to-all-start = ((bf16[8,2,8,3584]{3,2,1,0:T(8,128)(2,1)}), bf16[8,2,8,3584]{3,2,1,0:T(8,128)(2,1)S(1)}, u32[]{:S(2)}, u32[]{:S(2)}) async-start(bf16[8,2,8,3584]{3,2,1,0:T(8,128)(2,1)} %bitcast.15), calls=%async_computation | async-start | bytes 1835008 | tf_op jit(solution)/shard_map/all_to_all | solution.py:104
  49.4 1.3 dynamic_slice.3
  51.3 20.2 %all-to-all-done = bf16[8,2,8,3584]{3,2,1,0:T(8,128)(2,1)S(1)} async-done(((bf16[8,2,8,3584]{3,2,1,0:T(8,128)(2,1)}), bf16[8,2,8,3584]{3,2,1,0:T(8,128)(2,1)S(1)}, u32[]{:S(2)}, u32[]{:S(2)}) %all-to-all-start) | async-done | bytes 917536 | tf_op jit(solution)/shard_map/all_to_all | solution.py:104
  71.5 0.6 gather_fusion.2
  72.2 1.1 broadcast_select_fusion
  73.2 83.6 %all-gather.5.cloned.1.call-done = bf16[4096,512]{1,0:T(8,128)(2,1)} async-done(((bf16[128,512]{1,0:T(8,128)(2,1)}), bf16[4096,512]{1,0:T(8,128)(2,1)}) %all-gather.5.cloned.1.call-update) | async-done | bytes 4194320 | tf_op jit(solution)/shard_map/all_gather | solution.py:141
  156.8 6.4 %copy.42 = bf16[4096,512]{0,1:T(8,128)(2,1)} copy(bf16[4096,512]{1,0:T(8,128)(2,1)} %all-gather.5.cloned.1.call-done) | data formatting | bytes 8388608 | tf_op jit(solution)/shard_map/all_gather | solution.py:141
  163.2 102.9 %all-gather.3.cloned.1.call-done = bf16[4096,512]{1,0:T(8,128)(2,1)} async-done(((bf16[128,512]{1,0:T(8,128)(2,1)}), bf16[4096,512]{1,0:T(8,128)(2,1)}) %all-gather.3.cloned.1.call-update) | async-done | bytes 4194320 | tf_op jit(solution)/shard_map/all_gather | solution.py:140
  266.1 6.4 %copy.41 = bf16[4096,512]{0,1:T(8,128)(2,1)} copy(bf16[4096,512]{1,0:T(8,128)(2,1)} %all-gather.3.cloned.1.call-done) | data formatting | bytes 8388608 | tf_op jit(solution)/shard_map/all_gather | solution.py:140
  272.5 42.3 %conditional.2 = (f32[4,7,64]{2,1,0:T(8,128)S(1)}, f32[64,4,7,128]{3,0,2,1:T(8,128)}) conditional(s32[]{:T(128)} %convert_element_type.23, () %tuple.23, (s32[4096]{0:T(1024)S(1)}, s32[]{:T(128)}, s32[]{:T(128)}, s32[4096]{0:T(1024)S(1)}, bf16[16,8,3584]{2,1,0:T(8,128)(2,1)}, /*index=5*/bf16[4096,4,128]{0,2,1:T(8,128)(2,1)}, ...), branch_computations={%region_3.0_spmd, %region_4.9_spmd} | conditional | flops 3839363328 | bytes 117590584 | solution.py:61
  272.6 0.2 compare_and_fusion
  272.8 1.1 slice.8
  273.9 0.6 reshape.200
  274.5 13.9 %fusion = (f32[4,7,64]{2,1,0:T(8,128)S(1)}, f32[4,4096,64,7]{1,2,3,0:T(8,128)}) fusion(pred[64,4096]{1,0:T(8,128)(4,1)S(1)} %compare_and_fusion, bf16[64,4,7,128]{3,2,1,0:T(8,128)(2,1)S(1)} %reshape.200, bf16[4096,4,128]{0,2,1:T(8,128)(2,1)} %get-tuple-element.106), kind=kOutput, calls=%fused_computation.9 | convolution fusion | flops 1901066496 | bytes 34282496 | tf_op jit(solution)/shard_map/cond/branch_1_fun/rkgd,nkd->kgrn/dot_general | solution.py:42
  288.4 12.9 %fusion.11 = f32[64,4,7,128]{3,0,2,1:T(8,128)} fusion(bf16[4096,4,128]{0,2,1:T(8,128)(2,1)S(1)} %copy-done.2, f32[4,4096,64,7]{1,2,3,0:T(8,128)} %get-tuple-element.116, f32[4,7,64]{2,1,0:T(8,128)S(1)} %broadcast_maximum_fusion, pred[64,4096]{1,0:T(8,128)(4,1)S(1)} %compare_and_fusion), kind=kOutput, calls=%fused_computation.19 | convolution fusion | flops 1908408320 | bytes 34741248 | tf_op jit(solution)/shard_map/cond/branch_1_fun/kgrn,nkd->rkgd/dot_general | solution.py:52
  301.3 13.6 %fusion.4 = f32[4,7,64]{2,1,0:T(8,128)S(1)} fusion(f32[4,4096,64,7]{1,2,3,0:T(8,128)} %get-tuple-element.116, f32[4,7,64]{2,1,0:T(8,128)S(1)} %broadcast_maximum_fusion, pred[64,4096]{1,0:T(8,128)(4,1)S(1)} %compare_and_fusion), kind=kLoop, calls=%fused_computation.13 | loop fusion | flops 29358336 | bytes 29636608 | tf_op jit(solution)/shard_map/cond/branch_1_fun/reduce_sum | solution.py:51
  314.9 1.5 broadcast_divide_fusion.1
  316.4 0.3 copy.45
  316.7 0.5 reshape.226
  317.2 0.9 select_convert_fusion.1
  318.1 42.9 %conditional.3 = (f32[4,7,64]{2,1,0:T(8,128)}, f32[64,4,7,128]{3,0,2,1:T(8,128)}) conditional(s32[]{:T(128)} %convert_element_type.26, () %tuple.25, (s32[4096]{0:T(1024)S(1)}, s32[]{:T(128)}, s32[]{:T(128)}, s32[4096]{0:T(1024)S(1)}, bf16[16,8,3584]{2,1,0:T(8,128)(2,1)}, /*index=5*/bf16[4096,4,128]{0,2,1:T(8,128)(2,1)}, ...), branch_computations={%region_7.10_spmd, %region_8.13_spmd} | conditional | flops 3839363328 | bytes 117590584 | solution.py:61
  318.2 0.2 compare_and_fusion.1
  318.4 1.1 slice.9
  319.5 0.6 reshape.201
  320.0 0.0 copy-start.3
  320.0 13.9 %fusion.19 = (f32[4,7,64]{2,1,0:T(8,128)S(1)}, f32[4,4096,64,7]{1,2,3,0:T(8,128)}) fusion(pred[64,4096]{1,0:T(8,128)(4,1)S(1)} %compare_and_fusion.1, bf16[64,4,7,128]{3,2,1,0:T(8,128)(2,1)S(1)} %reshape.201, bf16[4096,4,128]{0,2,1:T(8,128)(2,1)} %get-tuple-element.113), kind=kOutput, calls=%fused_computation.29 | convolution fusion | flops 1901066496 | bytes 34282496 | tf_op jit(solution)/shard_map/cond/branch_1_fun/rkgd,nkd->kgrn/dot_general | solution.py:42
  334.0 0.0 copy-done.3
  334.0 12.9 %fusion.30 = f32[64,4,7,128]{3,0,2,1:T(8,128)} fusion(bf16[4096,4,128]{0,2,1:T(8,128)(2,1)S(1)} %copy-done.3, f32[4,4096,64,7]{1,2,3,0:T(8,128)} %get-tuple-element.118, f32[4,7,64]{2,1,0:T(8,128)S(1)} %broadcast_maximum_fusion.1, pred[64,4096]{1,0:T(8,128)(4,1)S(1)} %compare_and_fusion.1), kind=kOutput, calls=%fused_computation.39 | convolution fusion | flops 1908408320 | bytes 34741248 | tf_op jit(solution)/shard_map/cond/branch_1_fun/kgrn,nkd->rkgd/dot_general | solution.py:52
  346.9 14.2 %fusion.23 = f32[4,7,64]{2,1,0:T(8,128)} fusion(f32[4,4096,64,7]{1,2,3,0:T(8,128)} %get-tuple-element.118, f32[4,7,64]{2,1,0:T(8,128)S(1)} %broadcast_maximum_fusion.1, pred[64,4096]{1,0:T(8,128)(4,1)S(1)} %compare_and_fusion.1), kind=kLoop, calls=%fused_computation.33 | loop fusion | flops 29358336 | bytes 29636608 | tf_op jit(solution)/shard_map/cond/branch_1_fun/reduce_sum | solution.py:51
  361.1 0.8 select_bitcast_fusion.2
  361.9 1.5 broadcast_divide_fusion
  363.4 0.3 copy.48
  363.7 0.5 reshape.227
  364.2 0.1 select_convert_fusion
  364.3 2.0 maximum_bitcast_fusion
  (25 shorter events, 0.1 us)
Async XLA Ops:
  6.5 36.6 %copy-start = (bf16[1,16,8,3584]{3,2,1,0:T(8,128)(2,1)S(1)}, bf16[1,16,8,3584]{3,2,1,0:T(8,128)(2,1)}, u32[]{:S(2)}) copy-start(bf16[1,16,8,3584]{3,2,1,0:T(8,128)(2,1)} %param.14) | copy-start | bytes 2752516
  10.3 10.1 %all-to-all-start.1 = ((s32[8,1,2]{2,1,0:T(1,128)}), s32[8,1,2]{2,1,0:T(1,128)S(1)}, u32[]{:S(2)}, u32[]{:S(2)}) async-start(s32[8,1,2]{2,1,0:T(1,128)} %bitcast.13), calls=%async_computation.1 | async-start | bytes 8192 | tf_op jit(solution)/shard_map/all_to_all | solution.py:107
  20.4 10.4 %all-to-all-start.2 = ((bf16[8,2,8,512]{3,2,1,0:T(8,128)(2,1)}), bf16[8,2,8,512]{3,2,1,0:T(8,128)(2,1)S(1)}, u32[]{:S(2)}, u32[]{:S(2)}) async-start(bf16[8,2,8,512]{3,2,1,0:T(8,128)(2,1)} %bitcast.18), calls=%async_computation.2 | async-start | bytes 262144 | tf_op jit(solution)/shard_map/all_to_all | solution.py:105
  30.9 10.1 %all-to-all-start.3 = ((bf16[8,2,8,512]{3,2,1,0:T(8,128)(2,1)}), bf16[8,2,8,512]{3,2,1,0:T(8,128)(2,1)S(1)}, u32[]{:S(2)}, u32[]{:S(2)}) async-start(bf16[8,2,8,512]{3,2,1,0:T(8,128)(2,1)} %bitcast.23), calls=%async_computation.3 | async-start | bytes 262144 | tf_op jit(solution)/shard_map/all_to_all | solution.py:106
  35.3 121.5 %all-gather.5.cloned.1.call-start = ((), (), s32[]{:S(2)}) async-start(), calls=%async_computation.5 | async-start | bytes 4325376 | tf_op jit(solution)/shard_map/all_gather | solution.py:141
  42.4 223.7 %all-gather.3.cloned.1.call-start = ((), (), s32[]{:S(2)}) async-start(), calls=%async_computation.4 | async-start | bytes 4325376 | tf_op jit(solution)/shard_map/all_gather | solution.py:140
  44.8 26.7 %all-to-all-start = ((bf16[8,2,8,3584]{3,2,1,0:T(8,128)(2,1)}), bf16[8,2,8,3584]{3,2,1,0:T(8,128)(2,1)S(1)}, u32[]{:S(2)}, u32[]{:S(2)}) async-start(bf16[8,2,8,3584]{3,2,1,0:T(8,128)(2,1)} %bitcast.15), calls=%async_computation | async-start | bytes 1835008 | tf_op jit(solution)/shard_map/all_to_all | solution.py:104
  274.4 14.0 %copy-start.2 = (bf16[4096,4,128]{0,2,1:T(8,128)(2,1)S(1)}, bf16[4096,4,128]{0,2,1:T(8,128)(2,1)}, u32[]{:S(2)}) copy-start(bf16[4096,4,128]{0,2,1:T(8,128)(2,1)} %get-tuple-element.107) | copy-start | bytes 12582916 | tf_op jit(solution)/shard_map/cond
  320.0 14.0 %copy-start.3 = (bf16[4096,4,128]{0,2,1:T(8,128)(2,1)S(1)}, bf16[4096,4,128]{0,2,1:T(8,128)(2,1)}, u32[]{:S(2)}) copy-start(bf16[4096,4,128]{0,2,1:T(8,128)(2,1)} %get-tuple-element.114) | copy-start | bytes 12582916 | tf_op jit(solution)/shard_map/cond
  361.1 5.3 %copy-start.1 = (bf16[1,16,8,3584]{3,2,1,0:T(8,128)(2,1)S(1)}, bf16[1,16,8,3584]{3,2,1,0:T(8,128)(2,1)}, u32[]{:S(2)}) copy-start(bf16[1,16,8,3584]{3,2,1,0:T(8,128)(2,1)} %param.14) | copy-start | bytes 2752516
Sparse Core Ops, SparseCore 0:
  42.5 114.2 all-gather.4
  160.3 105.7 all-gather.2
where the time goes:
time: 374 us; the launch traced here: 373 us
  waiting for transfers between devices  217 us (58%)
  matrix products  53.7 us (14%)
  other arithmetic  41.9 us (11%)
  local copies, waits for them, and re-layouts  26.4 us (7%)
  starting transfers between devices  19.8 us (5%)
  between operations  14.2 us (4%)
    all_gather x1, waiting for transfers between devices, local(): lax.all_gather(local_k, 'ctx', axis=0, tiled=True)  103 us
    all_gather x1, waiting for transfers between devices, local(): lax.all_gather(local_v, 'ctx', axis=0, tiled=True)  83.6 us
    dot_general x2, matrix products, advance(): jnp.einsum('rkgd,nkd->kgrn', queries, key_rows, preferred_element_type=jn...  27.9 us
    reduce_sum x2, other arithmetic, advance(): weight_sum = jnp.sum(weights, axis=-1)  27.7 us
    dot_general x2, matrix products, advance(): jnp.einsum('kgrn,nkd->rkgd', weights.astype(jnp.bfloat16), value_rows, pr...  25.8 us
    all_to_all x1, waiting for transfers between devices, local(): lax.all_to_all(send_q, 'sec', split_axis=0, concat_axis=0, tiled=True)  20.2 us
  transfers between devices with their start and end apart: 6, of which 6 were waited for; matrix products, arithmetic and copies ran while one was open for 4% of the time, Pallas kernels for 0%

commit v1 on v0

v1 whole, which is shorter than its diff:
```python
import functools
import math

import jax
import jax.numpy as jnp
from jax import lax
from jax.experimental import pallas as pl
from jax.experimental.pallas import tpu as pltpu
from jax.sharding import Mesh, PartitionSpec as P

SEC = ("zl", "core")
BLOCK = 128
LANES = 128
GROUP = 7
HEADS_KV = 4
NEG = -1e30
VMEM_LIMIT = 56 * 1024 * 1024


def slot_order(sec_ref, order_ref, count_ref):
    for s in range(8):
        count_ref[s] = 0

    def body(i, _):
        s = sec_ref[0, i]
        c = count_ref[s]
        order_ref[2 * s + c] = i
        count_ref[s] = c + 1
        return 0

    lax.fori_loop(0, 16, body, 0)


def prep_kv_kernel(sec_ref, k_ref, v_ref, out_ref, order_ref, count_ref):
    slot_order(sec_ref, order_ref, count_ref)
    for s in range(8):
        a, b = order_ref[2 * s], order_ref[2 * s + 1]
        for row, ref in ((0, k_ref), (16, v_ref)):
            both = jnp.concatenate([ref[0, a], ref[0, b]], axis=0)
            for h in range(HEADS_KV):
                piece = both[:, h * LANES : (h + 1) * LANES]
                for zh in range(2):
                    out_ref[(zh * 4 + h) * 8 + s, row : row + 16, :] = piece


def prep_q_kernel(sec_ref, off_ref, q_ref, out_ref, order_ref, count_ref):
    slot_order(sec_ref, order_ref, count_ref)
    me = lax.axis_index("zl") * 2 + lax.axis_index("core")
    rel = lax.broadcasted_iota(jnp.int32, (8, LANES), 1) - 16 * me
    for s in range(8):
        a, b = order_ref[2 * s], order_ref[2 * s + 1]
        pos_a = jnp.bitwise_and(off_ref[0, a], BLOCK - 1)
        pos_b = jnp.bitwise_and(off_ref[0, b], BLOCK - 1)
        pos = jnp.where(rel < 8, pos_a + rel, pos_b + rel - 8)
        pos = jnp.where((rel >= 0) & (rel < 16), pos, 0)
        pos = pos.astype(jnp.float32).astype(jnp.bfloat16)
        both = jnp.concatenate([q_ref[0, a], q_ref[0, b]], axis=0)
        for h in range(HEADS_KV):
            for g in range(GROUP):
                col = (h * GROUP + g) * LANES
                out_ref[h * 8 + s, g * 16 : (g + 1) * 16, :] = both[:, col : col + LANES]
            out_ref[h * 8 + s, GROUP * 16 :, :] = pos


def attend_kernel(
    shifts,
    video_ref,
    q_ref,
    own_ref,
    prev_ref,
    next_ref,
    far0_ref,
    far1_ref,
    out_ref,
    kv_s,
    q_s,
    s_s,
    max_s,
    sum_s,
    acc_s,
    sem,
):
    x, y, zh = lax.axis_index("x"), lax.axis_index("y"), lax.axis_index("zh")
    me = lax.axis_index("zl") * 2 + lax.axis_index("core")
    live = video_ref[me] * 8
    rows = GROUP * BLOCK
    factor = math.log2(math.e) / math.sqrt(128.0)

    copies = []
    for a, ref in enumerate((own_ref, prev_ref, next_ref)):
        for zp in range(2):
            copies.append((ref.at[pl.ds(zp * 32, 32)], (zp * 4 + a) * 32))
    copies.append((far0_ref, 3 * 32))
    copies.append((far1_ref, 7 * 32))
    started = []
    for i, (src, at) in enumerate(copies):
        copy = pltpu.make_async_copy(src, kv_s.at[pl.ds(at, 32)], sem.at[i])
        copy.start()
        started.append(copy)
    for copy in started:
        copy.wait()

    row_pos = lax.broadcasted_iota(jnp.int32, (BLOCK, LANES), 0).astype(jnp.float32)

    def one_block(i, xb):
        block = zh * 16 + xb * 4 + y
        block_live = block * BLOCK < live

        @pl.when(jnp.logical_not(block_live))
        def _():
            out_ref[i] = jnp.zeros((BLOCK, rows), jnp.bfloat16)

        @pl.when(block_live)
        def _():
            meta = q_ref[pl.ds(xb * 8, 8), GROUP * 16 :, :].astype(jnp.float32)
            pos = jnp.sum(meta, axis=0)[0:1]
            pick = (row_pos == pos).astype(jnp.float32).astype(jnp.bfloat16)
            for g in range(GROUP):
                raw = q_ref[pl.ds(xb * 8, 8), g * 16 : (g + 1) * 16, :].reshape(BLOCK, LANES)
                q_s[g * BLOCK : (g + 1) * BLOCK, :] = jnp.dot(
                    pick, raw, preferred_element_type=jnp.float32
                ).astype(jnp.bfloat16)
            max_s[...] = jnp.full((rows, LANES), NEG, jnp.float32)
            sum_s[...] = jnp.zeros((rows, LANES), jnp.float32)
            acc_s[...] = jnp.zeros((rows, LANES), jnp.float32)
            alive = block * BLOCK + pos.astype(jnp.int32) < live
            diag_pos = jnp.where(alive, pos, 1e9)

            def scores(j, width, bounds):
                keys = kv_s[pl.ds(j * 32, width // 16), 0:16, :].reshape(width, LANES)
                s = lax.dot_general(
                    q_s[...], keys, (((1,), (1,)), ((), ())), preferred_element_type=jnp.float32
                )
                top = None
                for c in range(width // LANES):
                    part = s[:, c * LANES : (c + 1) * LANES]
                    if bounds is not None:
                        seen = (bounds[c] <= row_pos)[None]
                        part = jnp.where(
                            seen, part.reshape(GROUP, BLOCK, LANES), NEG
                        ).reshape(rows, LANES)
                    s_s[j, :, c * LANES : (c + 1) * LANES] = part
                    top = part if top is None else jnp.maximum(top, part)
                max_s[...] = jnp.maximum(max_s[...], top)

            def mix(j, width):
                values = kv_s[pl.ds(j * 32, width // 16), 16:32, :].reshape(width, LANES)
                top = max_s[...]
                parts, total = [], None
                for c in range(width // LANES):
                    p = jnp.exp2(s_s[j, :, c * LANES : (c + 1) * LANES] * factor - top)
                    total = p if total is None else total + p
                    parts.append(p.astype(jnp.bfloat16))
                sum_s[...] += total
                acc_s[...] += jnp.dot(
                    jnp.concatenate(parts, axis=1), values, preferred_element_type=jnp.float32
                )

            def each(full, part):
                @pl.when(zh == 1)
                def _():
                    lax.fori_loop(0, 4, lambda j, _: (full(j), 0)[1], 0)

                def own(a, _):
                    ya = jnp.bitwise_and(y + jnp.where(a == 0, 0, jnp.where(a == 1, 3, a - 1)), 3)
                    n = xb + (ya <= y).astype(jnp.int32)
                    part(zh * 4 + a, ya, n)
                    return 0

                lax.fori_loop(0, 4, own, 0)

            def part_scores(j, ya, n):
                bounds = []
                for xp in range(4):
                    all_seen = (xp < xb) | ((xp == xb) & (ya < y))
                    diag = (xp == xb) & (ya == y)
                    bound = jnp.where(diag, diag_pos, jnp.where(all_seen, -1.0, 1e9))
                    bounds.append(bound)

                @pl.when(n > 2)
                def _():
                    scores(j, 512, bounds)

                @pl.when((n > 0) & (n <= 2))
                def _():
                    scores(j, 256, bounds)

            def part_mix(j, ya, n):
                @pl.when(n > 2)
                def _():
                    mix(j, 512)

                @pl.when((n > 0) & (n <= 2))
                def _():
                    mix(j, 256)

            each(lambda j: scores(j, 512, None), part_scores)
            top = jnp.max(max_s[...], axis=1, keepdims=True) * factor
            max_s[...] = jnp.broadcast_to(top, (rows, LANES))
            each(lambda j: mix(j, 512), part_mix)
            total = jnp.sum(sum_s[...], axis=1, keepdims=True)
            out = acc_s[...] / total
            row_live = row_pos < (live - block * BLOCK).astype(jnp.float32)
            for g in range(GROUP):
                piece = jnp.where(row_live, out[g * BLOCK : (g + 1) * BLOCK], 0.0)
                out_ref[i, :, g * LANES : (g + 1) * LANES] = piece.astype(jnp.bfloat16)

    for i, shift in enumerate(shifts):
        one_block(i, jnp.bitwise_and(x + shift, 3))


def join_kernel(a_ref, b_ref, c_ref, d_ref, out_ref, sem):
    x = lax.axis_index("x")
    copies = []
    for k, ref in enumerate((a_ref, b_ref, c_ref, d_ref)):
        head = jnp.bitwise_and(x + 4 - k, 3)
        col = pl.multiple_of(head * (GROUP * LANES), LANES)
        copy = pltpu.make_async_copy(
            ref.at[0], out_ref.at[0, :, pl.ds(col, GROUP * LANES)], sem.at[k]
        )
        copy.start()
        copies.append(copy)
    for copy in copies:
        copy.wait()


def vmem():
    return pl.BlockSpec(memory_space=pltpu.VMEM)


def smem():
    return pl.BlockSpec(memory_space=pltpu.SMEM)


def anywhere():
    return pl.BlockSpec(memory_space=pl.ANY)


def params():
    return pltpu.CompilerParams(vmem_limit_bytes=VMEM_LIMIT)


def exchange(value, axes):
    return lax.all_to_all(value, axes, split_axis=0, concat_axis=0, tiled=True)


def shift(value, axis, by):
    return lax.ppermute(value, axis, [(i, (i + by) % 4) for i in range(4)])


def local(q_frames, k_frames, v_frames, video_frames, frame_section, frame_offset):
    order = [pltpu.SMEM((16,), jnp.int32), pltpu.SMEM((8,), jnp.int32)]
    kv_send = pl.pallas_call(
        prep_kv_kernel,
        out_shape=jax.ShapeDtypeStruct((64, 32, LANES), jnp.bfloat16),
        in_specs=[smem(), vmem(), vmem()],
        out_specs=vmem(),
        scratch_shapes=order,
        compiler_params=params(),
        name="prep_kv",
    )(frame_section, k_frames, v_frames)
    q_send = pl.pallas_call(
        prep_q_kernel,
        out_shape=jax.ShapeDtypeStruct((32, GROUP * 16 + 8, LANES), jnp.bfloat16),
        in_specs=[smem(), smem(), vmem()],
        out_specs=vmem(),
        scratch_shapes=order,
        compiler_params=params(),
        name="prep_q",
    )(frame_section, frame_offset, q_frames)
    own = exchange(kv_send, ("zh", "x", "zl", "core"))
    q_send, own = lax.optimization_barrier((q_send, own))
    q_got = exchange(q_send, ("x", "zl", "core"))
    prev, nxt = shift(own, "y", 1), shift(own, "y", -1)
    far0, far1 = shift(prev[:32], "y", 1), shift(nxt[32:], "y", -1)

    def attend(shifts):
        rows = GROUP * BLOCK
        return pl.pallas_call(
            functools.partial(attend_kernel, shifts),
            out_shape=jax.ShapeDtypeStruct((len(shifts), BLOCK, rows), jnp.bfloat16),
            in_specs=[smem(), vmem()] + [anywhere()] * 5,
            out_specs=vmem(),
            scratch_shapes=[
                pltpu.VMEM((256, 32, LANES), jnp.bfloat16),
                pltpu.VMEM((rows, LANES), jnp.bfloat16),
                pltpu.VMEM((8, rows, 512), jnp.float32),
                pltpu.VMEM((rows, LANES), jnp.float32),
                pltpu.VMEM((rows, LANES), jnp.float32),
                pltpu.VMEM((rows, LANES), jnp.float32),
                pltpu.SemaphoreType.DMA((8,)),
            ],
            compiler_params=params(),
            cost_estimate=pl.CostEstimate(
                flops=2 * 2 * rows * 4096 * LANES,
                transcendentals=rows * 4096,
                bytes_accessed=3 << 20,
            ),
            name="attend",
        )(video_frames, q_got, own, prev, nxt, far0, far1)

    parts = {}
    for k in (1, 2, 3, 0):
        part = attend((k,))
        parts[k] = shift(part, "x", k) if k else part
    return pl.pallas_call(
        join_kernel,
        out_shape=jax.ShapeDtypeStruct((1, BLOCK, HEADS_KV * GROUP * LANES), jnp.bfloat16),
        in_specs=[anywhere()] * 4,
        out_specs=anywhere(),
        scratch_shapes=[pltpu.SemaphoreType.DMA((4,))],
        compiler_params=params(),
        name="join",
    )(parts[0], parts[1], parts[2], parts[3])


def solution(mesh):
    fine = Mesh(mesh.devices.reshape(4, 2, 2, 4, 4), ("zl", "core", "zh", "x", "y"))
    ctx = ("zh", "x", "y")
    return jax.shard_map(
        local,
        mesh=fine,
        in_specs=(
            P(SEC, ctx, None, None),
            P(SEC, ctx, None, None),
            P(SEC, ctx, None, None),
            P(),
            P(SEC, ctx),
            P(SEC, ctx),
        ),
        out_specs=P(SEC, ctx, None),
        check_vma=False,
    )
```

time: 374 us -> 140 us (0.37)
  the two profiles are of different devices: /device:TPU:32 before, /device:TPU:128 now
where the time goes in v1:
time: 140 us; the launch traced here: 139 us
  Pallas kernels  73.2 us (52%)
  waiting for transfers between devices  32.5 us (23%)
  starting transfers between devices  29.4 us (21%)
  local copies, waits for them, and re-layouts  3.12 us (2%)
    pallas_call x4, Pallas kernels, attend(): pl.pallas_call(functools.partial(attend_kernel, shifts), out_shape=jax.Sh...  39.7 us
    pallas_call x1, Pallas kernels, local(): pl.pallas_call(join_kernel, out_shape=jax.ShapeDtypeStruct((1, BLOCK, HEA...  28.9 us
    ppermute x7, waiting for transfers between devices, shift(): return lax.ppermute(value, axis, [(i, (i + by) % 4) for i in range(4)])  20.2 us
    all_to_all x2, starting transfers between devices, exchange(): return lax.all_to_all(value, axes, split_axis=0, concat_axis=0, tiled=True)  15.4 us
    ppermute x7, starting transfers between devices, shift(): return lax.ppermute(value, axis, [(i, (i + by) % 4) for i in range(4)])  14 us
    all_to_all x2, waiting for transfers between devices, exchange(): return lax.all_to_all(value, axes, split_axis=0, concat_axis=0, tiled=True)  12.3 us
    unnamed x18, local copies, waits for them, and re-layouts  3.08 us
  transfers between devices with their start and end apart: 9, of which 4 were waited for; matrix products, arithmetic and copies ran while one was open for 0% of the time, Pallas kernels for 23%

profile of v1, /device:TPU:128, one launch (start us, length us, event | category | flops | bytes accessed | tf_op | source)
XLA Modules:
  0.0 138.5 jit_solution(17605366116057069294)
XLA Ops:
  0.0 2.1 %prep_kv.1 = bf16[64,32,128]{2,1,0:T(8,128)(2,1)} custom-call(s32[1,16]{1,0:T(1,128)} %sec_ref.3, bf16[1,16,8,512]{3,2,1,0:T(8,128)(2,1)} %k_ref.1, bf16[1,16,8,512]{3,2,1,0:T(8,128)(2,1)} %v_ref.1), custom_call_target="tpu_custom_call" | custom-call | tf_op jit(solution)/shard_map/prep_kv/pallas_call | solution.py:253
  2.1 10.3 %all-to-all-start = ((bf16[64,32,128]{2,1,0:T(8,128)(2,1)}), bf16[64,32,128]{2,1,0:T(8,128)(2,1)S(1)}, u32[]{:S(2)}, u32[]{:S(2)}) async-start(bf16[64,32,128]{2,1,0:T(8,128)(2,1)} %prep_kv.1), calls=%async_computation | async-start | bytes 1048576 | tf_op jit(solution)/shard_map/all_to_all | solution.py:244
  12.4 2.6 %prep_q.1 = bf16[32,120,128]{2,1,0:T(8,128)(2,1)} custom-call(s32[1,16]{1,0:T(1,128)} %sec_ref.3, s32[1,16]{1,0:T(1,128)} %off_ref.1, bf16[1,16,8,3584]{3,2,1,0:T(8,128)(2,1)} %q_ref.1), custom_call_target="tpu_custom_call" | custom-call | tf_op jit(solution)/shard_map/prep_q/pallas_call | solution.py:262
  14.9 12.3 %all-to-all-done.own_ref = bf16[64,32,128]{2,1,0:T(8,128)(2,1)S(1)} async-done(((bf16[64,32,128]{2,1,0:T(8,128)(2,1)}), bf16[64,32,128]{2,1,0:T(8,128)(2,1)S(1)}, u32[]{:S(2)}, u32[]{:S(2)}) %all-to-all-start) | async-done | bytes 524320 | tf_op jit(solution)/shard_map/all_to_all | solution.py:244
  27.3 0.0 copy-start.1
  27.3 5.0 %all-to-all-start.1 = ((bf16[32,120,128]{2,1,0:T(8,128)(2,1)}), bf16[32,120,128]{2,1,0:T(8,128)(2,1)S(1)}, u32[]{:S(2)}, u32[]{:S(2)}) async-start(bf16[32,120,128]{2,1,0:T(8,128)(2,1)} %prep_q.1), calls=%async_computation.1 | async-start | bytes 1966080 | tf_op jit(solution)/shard_map/all_to_all | solution.py:244
  32.3 3.1 %collective-permute-start.1 = (bf16[64,32,128]{2,1,0:T(8,128)(2,1)S(1)}, bf16[64,32,128]{2,1,0:T(8,128)(2,1)S(1)}, u32[]{:S(2)}, u32[]{:S(2)}) collective-permute-start(bf16[64,32,128]{2,1,0:T(8,128)(2,1)S(1)} %all-to-all-done.own_ref), channel_id=1, source_target_pairs={{0,3},{1,0},{2,1},{3,2},{4,7},{5,4},{6,5},{7,6},{8,11},{9,8},{10,9... | collective-permute-start | bytes 1572872 | tf_op jit(solution)/shard_map/ppermute | solution.py:248
  35.4 0.0 copy-done.1
  35.4 0.0 collective-permute-start
  35.4 11.6 %collective-permute-done.1.next_ref = bf16[64,32,128]{2,1,0:T(8,128)(2,1)S(1)} collective-permute-done((bf16[64,32,128]{2,1,0:T(8,128)(2,1)S(1)}, bf16[64,32,128]{2,1,0:T(8,128)(2,1)S(1)}, u32[]{:S(2)}, u32[]{:S(2)}) %collective-permute-start.1) | collective-permute-done | bytes 524320 | tf_op jit(solution)/shard_map/ppermute | solution.py:248
  47.0 0.0 copy-start.5
  47.0 3.8 %collective-permute-start.3 = (bf16[32,32,128]{2,1,0:T(8,128)(2,1)S(1)}, bf16[32,32,128]{2,1,0:T(8,128)(2,1)S(1)}, u32[]{:S(2)}, u32[]{:S(2)}) collective-permute-start(bf16[32,32,128]{2,1,0:T(8,128)(2,1)S(1)} %slice.9), channel_id=1, source_target_pairs={{0,3},{1,0},{2,1},{3,2},{4,7},{5,4},{6,5},{7,6},{8,11},{9,8},{10,9... | collective-permute-start | bytes 786440 | tf_op jit(solution)/shard_map/ppermute | solution.py:248
  50.8 0.0 collective-permute-done.prev_ref
  50.8 0.0 copy-start.6
  50.8 0.0 copy-done.5
  50.8 0.1 collective-permute-start.2
  50.9 5.1 %collective-permute-done.3.far1_ref = bf16[32,32,128]{2,1,0:T(8,128)(2,1)S(1)} collective-permute-done((bf16[32,32,128]{2,1,0:T(8,128)(2,1)S(1)}, bf16[32,32,128]{2,1,0:T(8,128)(2,1)S(1)}, u32[]{:S(2)}, u32[]{:S(2)}) %collective-permute-start.3) | collective-permute-done | bytes 262176 | tf_op jit(solution)/shard_map/ppermute | solution.py:248
  56.0 0.0 copy-start.7
  56.0 3.5 %collective-permute-done.2.far0_ref = bf16[32,32,128]{2,1,0:T(8,128)(2,1)S(1)} collective-permute-done((bf16[32,32,128]{2,1,0:T(8,128)(2,1)S(1)}, bf16[32,32,128]{2,1,0:T(8,128)(2,1)S(1)}, u32[]{:S(2)}, u32[]{:S(2)}) %collective-permute-start.2) | collective-permute-done | bytes 262176 | tf_op jit(solution)/shard_map/ppermute | solution.py:248
  59.5 0.0 copy-start.8
  59.5 0.0 all-to-all-done.1.q_ref
  59.5 0.0 copy-done.6
  59.5 0.0 copy-done.7
  59.5 0.7 copy-done.8
  60.2 0.0 copy-start
  60.2 1.0 copy-done
  61.2 9.9 %attend.5 = bf16[1,128,896]{2,1,0:T(8,128)(2,1)} custom-call(s32[8]{0:T(128)} %video_ref.7, bf16[32,120,128]{2,1,0:T(8,128)(2,1)} %copy-done, bf16[64,32,128]{2,1,0:T(8,128)(2,1)} %copy-done.1, bf16[64,32,128]{2,1,0:T(8,128)(2,1)} %copy-done.6, bf16[64,32,128]{2,1,0:T(8,128)(2,1)} %copy-done.5, bf16[32,32,128]{2,1,0:T(8,128)(2,1)} %copy-done.8, ...), custom_call_target="tpu_custom_call" | custom-call | flops 1879048192 | bytes 3145728 | tf_op jit(solution)/shard_map/attend/pallas_call | solution.py:279
  71.1 1.9 %collective-permute-start.4 = (bf16[1,128,896]{2,1,0:T(8,128)(2,1)}, bf16[1,128,896]{2,1,0:T(8,128)(2,1)S(1)}, u32[]{:S(2)}, u32[]{:S(2)}) collective-permute-start(bf16[1,128,896]{2,1,0:T(8,128)(2,1)} %attend.5), channel_id=1, source_target_pairs={{0,4},{4,8},{8,12},{12,0},{1,5},{5,9},{9,13},{13,1},{2,6},{6,10},{... | collective-permute-start | bytes 688136 | tf_op jit(solution)/shard_map/ppermute | solution.py:248
  73.0 10.3 %attend.6 = bf16[1,128,896]{2,1,0:T(8,128)(2,1)} custom-call(s32[8]{0:T(128)} %video_ref.7, bf16[32,120,128]{2,1,0:T(8,128)(2,1)} %copy-done, bf16[64,32,128]{2,1,0:T(8,128)(2,1)} %copy-done.1, bf16[64,32,128]{2,1,0:T(8,128)(2,1)} %copy-done.6, bf16[64,32,128]{2,1,0:T(8,128)(2,1)} %copy-done.5, bf16[32,32,128]{2,1,0:T(8,128)(2,1)} %copy-done.8, ...), custom_call_target="tpu_custom_call" | custom-call | flops 1879048192 | bytes 3145728 | tf_op jit(solution)/shard_map/attend/pallas_call | solution.py:279
  83.3 0.5 collective-permute-start.5
  83.7 11.3 %attend.7 = bf16[1,128,896]{2,1,0:T(8,128)(2,1)} custom-call(s32[8]{0:T(128)} %video_ref.7, bf16[32,120,128]{2,1,0:T(8,128)(2,1)} %copy-done, bf16[64,32,128]{2,1,0:T(8,128)(2,1)} %copy-done.1, bf16[64,32,128]{2,1,0:T(8,128)(2,1)} %copy-done.6, bf16[64,32,128]{2,1,0:T(8,128)(2,1)} %copy-done.5, bf16[32,32,128]{2,1,0:T(8,128)(2,1)} %copy-done.8, ...), custom_call_target="tpu_custom_call" | custom-call | flops 1879048192 | bytes 3145728 | tf_op jit(solution)/shard_map/attend/pallas_call | solution.py:279
  95.0 4.7 %collective-permute-start.6 = (bf16[1,128,896]{2,1,0:T(8,128)(2,1)}, bf16[1,128,896]{2,1,0:T(8,128)(2,1)S(1)}, u32[]{:S(2)}, u32[]{:S(2)}) collective-permute-start(bf16[1,128,896]{2,1,0:T(8,128)(2,1)} %attend.7), channel_id=1, source_target_pairs={{0,12},{4,0},{8,4},{12,8},{1,13},{5,1},{9,5},{13,9},{2,14},{6,2},{... | collective-permute-start | bytes 688136 | tf_op jit(solution)/shard_map/ppermute | solution.py:248
  99.7 8.3 %attend.4.a_ref = bf16[1,128,896]{2,1,0:T(8,128)(2,1)} custom-call(s32[8]{0:T(128)} %video_ref.7, bf16[32,120,128]{2,1,0:T(8,128)(2,1)} %copy-done, bf16[64,32,128]{2,1,0:T(8,128)(2,1)} %copy-done.1, bf16[64,32,128]{2,1,0:T(8,128)(2,1)} %copy-done.6, bf16[64,32,128]{2,1,0:T(8,128)(2,1)} %copy-done.5, bf16[32,32,128]{2,1,0:T(8,128)(2,1)} %copy-done.8, ...), custom_call_target="tpu_custom_call" | custom-call | flops 1879048192 | bytes 3145728 | tf_op jit(solution)/shard_map/attend/pallas_call | solution.py:279
  108.0 0.0 collective-permute-done.4.b_ref
  108.0 0.0 copy-start.2
  108.0 0.0 collective-permute-done.5.c_ref
  108.0 0.0 copy-start.3
  108.0 0.0 collective-permute-done.6.d_ref
  108.0 0.6 copy-done.2
  108.7 0.1 copy-done.3
  108.8 0.0 copy-start.4
  108.8 0.7 copy-done.4
  109.4 28.9 %join.1 = bf16[1,128,3584]{2,1,0:T(8,128)(2,1)} custom-call(bf16[1,128,896]{2,1,0:T(8,128)(2,1)} %attend.4.a_ref, bf16[1,128,896]{2,1,0:T(8,128)(2,1)} %copy-done.2, bf16[1,128,896]{2,1,0:T(8,128)(2,1)} %copy-done.3, bf16[1,128,896]{2,1,0:T(8,128)(2,1)} %copy-done.4), custom_call_target="tpu_custom_call" | custom-call | tf_op jit(solution)/shard_map/join/pallas_call | solution.py:306
  (2 shorter events, 0.0 us)
Async XLA Ops:
  2.1 25.2 %all-to-all-start = ((bf16[64,32,128]{2,1,0:T(8,128)(2,1)}), bf16[64,32,128]{2,1,0:T(8,128)(2,1)S(1)}, u32[]{:S(2)}, u32[]{:S(2)}) async-start(bf16[64,32,128]{2,1,0:T(8,128)(2,1)} %prep_kv.1), calls=%async_computation | async-start | bytes 1048576 | tf_op jit(solution)/shard_map/all_to_all | solution.py:244
  27.3 8.1 %copy-start.1 = (bf16[64,32,128]{2,1,0:T(8,128)(2,1)}, bf16[64,32,128]{2,1,0:T(8,128)(2,1)S(1)}, u32[]{:S(2)}) copy-start(bf16[64,32,128]{2,1,0:T(8,128)(2,1)S(1)} %all-to-all-done.own_ref) | copy-start | bytes 1572868
  27.3 32.3 %all-to-all-start.1 = ((bf16[32,120,128]{2,1,0:T(8,128)(2,1)}), bf16[32,120,128]{2,1,0:T(8,128)(2,1)S(1)}, u32[]{:S(2)}, u32[]{:S(2)}) async-start(bf16[32,120,128]{2,1,0:T(8,128)(2,1)} %prep_q.1), calls=%async_computation.1 | async-start | bytes 1966080 | tf_op jit(solution)/shard_map/all_to_all | solution.py:244
  32.3 14.7 %collective-permute-start.1 = (bf16[64,32,128]{2,1,0:T(8,128)(2,1)S(1)}, bf16[64,32,128]{2,1,0:T(8,128)(2,1)S(1)}, u32[]{:S(2)}, u32[]{:S(2)}) collective-permute-start(bf16[64,32,128]{2,1,0:T(8,128)(2,1)S(1)} %all-to-all-done.own_ref), channel_id=1, source_target_pairs={{0,3},{1,0},{2,1},{3,2},{4,7},{5,4},{6,5},{7,6},{8,11},{9,8},{10,9... | collective-permute-start | bytes 1572872 | tf_op jit(solution)/shard_map/ppermute | solution.py:248
  35.4 15.4 %collective-permute-start = (bf16[64,32,128]{2,1,0:T(8,128)(2,1)S(1)}, bf16[64,32,128]{2,1,0:T(8,128)(2,1)S(1)}, u32[]{:S(2)}, u32[]{:S(2)}) collective-permute-start(bf16[64,32,128]{2,1,0:T(8,128)(2,1)S(1)} %all-to-all-done.own_ref), channel_id=1, source_target_pairs={{0,1},{1,2},{2,3},{3,0},{4,5},{5,6},{6,7},{7,4},{8,9},{9,10},{10,1... | collective-permute-start | bytes 1572872 | tf_op jit(solution)/shard_map/ppermute | solution.py:248
  47.0 3.8 %copy-start.5 = (bf16[64,32,128]{2,1,0:T(8,128)(2,1)}, bf16[64,32,128]{2,1,0:T(8,128)(2,1)S(1)}, u32[]{:S(2)}) copy-start(bf16[64,32,128]{2,1,0:T(8,128)(2,1)S(1)} %collective-permute-done.1.next_ref) | copy-start | bytes 1572868
  47.0 9.0 %collective-permute-start.3 = (bf16[32,32,128]{2,1,0:T(8,128)(2,1)S(1)}, bf16[32,32,128]{2,1,0:T(8,128)(2,1)S(1)}, u32[]{:S(2)}, u32[]{:S(2)}) collective-permute-start(bf16[32,32,128]{2,1,0:T(8,128)(2,1)S(1)} %slice.9), channel_id=1, source_target_pairs={{0,3},{1,0},{2,1},{3,2},{4,7},{5,4},{6,5},{7,6},{8,11},{9,8},{10,9... | collective-permute-start | bytes 786440 | tf_op jit(solution)/shard_map/ppermute | solution.py:248
  50.8 8.7 %copy-start.6 = (bf16[64,32,128]{2,1,0:T(8,128)(2,1)}, bf16[64,32,128]{2,1,0:T(8,128)(2,1)S(1)}, u32[]{:S(2)}) copy-start(bf16[64,32,128]{2,1,0:T(8,128)(2,1)S(1)} %collective-permute-done.prev_ref) | copy-start | bytes 1572868
  50.8 8.7 %collective-permute-start.2 = (bf16[32,32,128]{2,1,0:T(8,128)(2,1)S(1)}, bf16[32,32,128]{2,1,0:T(8,128)(2,1)S(1)}, u32[]{:S(2)}, u32[]{:S(2)}) collective-permute-start(bf16[32,32,128]{2,1,0:T(8,128)(2,1)S(1)} %slice.8), channel_id=1, source_target_pairs={{0,1},{1,2},{2,3},{3,0},{4,5},{5,6},{6,7},{7,4},{8,9},{9,10},{10,1... | collective-permute-start | bytes 786440 | tf_op jit(solution)/shard_map/ppermute | solution.py:248
  56.0 3.5 %copy-start.7 = (bf16[32,32,128]{2,1,0:T(8,128)(2,1)}, bf16[32,32,128]{2,1,0:T(8,128)(2,1)S(1)}, u32[]{:S(2)}) copy-start(bf16[32,32,128]{2,1,0:T(8,128)(2,1)S(1)} %collective-permute-done.3.far1_ref) | copy-start | bytes 786436
  59.5 0.7 copy-start.8
  60.2 1.0 copy-start
  71.1 36.9 %collective-permute-start.4 = (bf16[1,128,896]{2,1,0:T(8,128)(2,1)}, bf16[1,128,896]{2,1,0:T(8,128)(2,1)S(1)}, u32[]{:S(2)}, u32[]{:S(2)}) collective-permute-start(bf16[1,128,896]{2,1,0:T(8,128)(2,1)} %attend.5), channel_id=1, source_target_pairs={{0,4},{4,8},{8,12},{12,0},{1,5},{5,9},{9,13},{13,1},{2,6},{6,10},{... | collective-permute-start | bytes 688136 | tf_op jit(solution)/shard_map/ppermute | solution.py:248
  83.3 24.7 %collective-permute-start.5 = (bf16[1,128,896]{2,1,0:T(8,128)(2,1)}, bf16[1,128,896]{2,1,0:T(8,128)(2,1)S(1)}, u32[]{:S(2)}, u32[]{:S(2)}) collective-permute-start(bf16[1,128,896]{2,1,0:T(8,128)(2,1)} %attend.6), channel_id=1, source_target_pairs={{0,8},{4,12},{8,0},{12,4},{1,9},{5,13},{9,1},{13,5},{2,10},{6,14},... | collective-permute-start | bytes 688136 | tf_op jit(solution)/shard_map/ppermute | solution.py:248
  95.0 13.0 %collective-permute-start.6 = (bf16[1,128,896]{2,1,0:T(8,128)(2,1)}, bf16[1,128,896]{2,1,0:T(8,128)(2,1)S(1)}, u32[]{:S(2)}, u32[]{:S(2)}) collective-permute-start(bf16[1,128,896]{2,1,0:T(8,128)(2,1)} %attend.7), channel_id=1, source_target_pairs={{0,12},{4,0},{8,4},{12,8},{1,13},{5,1},{9,5},{13,9},{2,14},{6,2},{... | collective-permute-start | bytes 688136 | tf_op jit(solution)/shard_map/ppermute | solution.py:248
  108.0 0.7 copy-start.2
  108.0 0.7 copy-start.3
  108.8 0.7 copy-start.4

commit v2 on v1

v2 whole, which is shorter than its diff:
```python
import functools
import math

import jax
import jax.numpy as jnp
from jax import lax
from jax.experimental import pallas as pl
from jax.experimental.pallas import tpu as pltpu
from jax.sharding import Mesh, PartitionSpec as P

SEC = ("zl", "core")
BLOCK = 128
LANES = 128
GROUP = 7
HEADS_KV = 4
NEG = -1e30
VMEM_LIMIT = 24 * 1024 * 1024
VMEM_ALL = 56 * 1024 * 1024
TILE = 512


def slot_order(sec_ref, order_ref, count_ref):
    for s in range(8):
        count_ref[s] = 0

    def body(i, _):
        s = sec_ref[0, i]
        c = count_ref[s]
        order_ref[2 * s + c] = i
        count_ref[s] = c + 1
        return 0

    lax.fori_loop(0, 16, body, 0)


def prep_kv_kernel(sec_ref, k_ref, v_ref, out_ref, order_ref, count_ref):
    slot_order(sec_ref, order_ref, count_ref)
    for s in range(8):
        a, b = order_ref[2 * s], order_ref[2 * s + 1]
        for row, ref in ((0, k_ref), (16, v_ref)):
            both = jnp.concatenate([ref[0, a], ref[0, b]], axis=0)
            for h in range(HEADS_KV):
                for zh in range(2):
                    out_ref[(zh * 4 + h) * 8 + s, row : row + 16, :] = both[:, h * LANES : (h + 1) * LANES]


def prep_q_kernel(sec_ref, off_ref, q_ref, out_ref, order_ref, count_ref):
    slot_order(sec_ref, order_ref, count_ref)
    me = lax.axis_index("zl") * 2 + lax.axis_index("core")
    rel = lax.broadcasted_iota(jnp.int32, (8, LANES), 1) - 16 * me
    for s in range(8):
        a, b = order_ref[2 * s], order_ref[2 * s + 1]
        pos_a = jnp.bitwise_and(off_ref[0, a], BLOCK - 1)
        pos_b = jnp.bitwise_and(off_ref[0, b], BLOCK - 1)
        pos = jnp.where(rel < 8, pos_a + rel, pos_b + rel - 8)
        pos = jnp.where((rel >= 0) & (rel < 16), pos, 0)
        pos = pos.astype(jnp.float32).astype(jnp.bfloat16)
        both = jnp.concatenate([q_ref[0, a], q_ref[0, b]], axis=0)
        for h in range(HEADS_KV):
            for g in range(GROUP):
                col = (h * GROUP + g) * LANES
                out_ref[h * 8 + s, g * 16 : (g + 1) * 16, :] = both[:, col : col + LANES]
            out_ref[h * 8 + s, GROUP * 16 :, :] = pos


def arrange_kernel(*refs):
    sources, kv_ref = refs[:5], refs[5]
    copies = []
    for p in range(2):
        own, prev, nxt, far_k, far_v = sources
        for xp in range(4):
            at = pl.ds((p * 4 + xp) * 8, 8)
            for a, src in enumerate((own, prev, nxt)):
                copies.append((src.at[at], kv_ref.at[p * 4 + xp, a]))
            copies.append((far_k.at[at], kv_ref.at[p * 4 + xp, 3, :, 0:16]))
            copies.append((far_v.at[at], kv_ref.at[p * 4 + xp, 3, :, 16:32]))
    for src, dst in copies:
        dst[...] = src[...]


def attend_kernel(
    shifts, video_ref, q_ref, kv_ref, *refs
):
    out_refs = refs[: len(shifts)]
    q_s, mask_s, s0, s1, top0, top1, max_s, sum_s, acc_s = refs[len(shifts) :]
    x, y, zh = lax.axis_index("x"), lax.axis_index("y"), lax.axis_index("zh")
    me = lax.axis_index("zl") * 2 + lax.axis_index("core")
    live = video_ref[me] * 8
    rows = GROUP * BLOCK
    factor = math.log2(math.e) / math.sqrt(128.0)
    down = lax.broadcasted_iota(jnp.int32, (BLOCK, LANES), 0)
    across = lax.broadcasted_iota(jnp.int32, (BLOCK, LANES), 1)

    def dot(a, b, ca, cb):
        return lax.dot_general(
            a, b, (((ca,), (cb,)), ((), ())), preferred_element_type=jnp.float32
        )

    def scores(t, s_ref, top_ref):
        s = dot(kv_ref[t, :, :, 0:16, :].reshape(TILE, LANES), q_s[...], 1, 0)
        s_ref[...] = s
        top_ref[...] = jnp.max(s.reshape(TILE // 8, 8, rows), axis=0)

    def absorb(t, s, top):
        old = max_s[...]
        new = jnp.maximum(old, jnp.max(top, axis=0, keepdims=True) * factor)
        keep = jnp.exp2(old - new)
        max_s[...] = new
        p = jnp.exp2(s * factor - new)
        sum_s[...] = sum_s[...] * keep + jnp.sum(p, axis=0, keepdims=True)
        mixed = dot(kv_ref[t, :, :, 16:32, :].reshape(TILE, LANES), p.astype(jnp.bfloat16), 0, 0)
        acc_s[...] = acc_s[...] * keep + mixed

    def absorb_last(t, s_ref):
        s = s_ref[...] + jnp.concatenate([mask_s[...]] * GROUP, axis=1)
        absorb(t, s, jnp.max(s.reshape(TILE // 8, 8, rows), axis=0))

    def one_block(out_ref, xb):
        block = zh * 16 + xb * 4 + y
        block_live = block * BLOCK < live

        @pl.when(jnp.logical_not(block_live))
        def _():
            out_ref[0] = jnp.zeros((BLOCK, rows), jnp.bfloat16)

        @pl.when(block_live)
        def _():
            first = 0
            last = zh * 4 + xb
            meta = q_ref[pl.ds(xb * 8, 8), GROUP * 16 :, :].astype(jnp.float32)
            pos = jnp.sum(meta, axis=0)[0:1]
            pick = (down.astype(jnp.float32) == pos).astype(jnp.float32).astype(jnp.bfloat16)
            for g in range(GROUP):
                raw = q_ref[pl.ds(xb * 8, 8), g * 16 : (g + 1) * 16, :].reshape(BLOCK, LANES)
                q_s[:, g * BLOCK : (g + 1) * BLOCK] = dot(raw, pick, 0, 1).astype(jnp.bfloat16)
            reach = (down <= across) & (block * BLOCK + down < live)
            seen = dot(pick, reach.astype(jnp.float32).astype(jnp.bfloat16), 0, 0)
            mask_s[0:BLOCK, :] = jnp.where(seen > 0.5, 0.0, NEG)
            for a, by in ((1, 3), (2, 1), (3, 2)):
                before = jnp.bitwise_and(y + by, 3) < y
                mask_s[a * BLOCK : (a + 1) * BLOCK, :] = jnp.full(
                    (BLOCK, LANES), jnp.where(before, 0.0, NEG)
                )
            max_s[...] = jnp.full((1, rows), NEG, jnp.float32)
            sum_s[...] = jnp.zeros((1, rows), jnp.float32)
            acc_s[...] = jnp.zeros((LANES, rows), jnp.float32)

            scores(first, s0, top0)
            full = last - first

            def pair(n, _):
                t = first + 2 * n
                scores(t + 1, s1, top1)
                absorb(t, s0[...], top0[...])
                scores(t + 2, s0, top0)
                absorb(t + 1, s1[...], top1[...])
                return 0

            lax.fori_loop(0, lax.shift_right_logical(full, 1), pair, 0)
            odd = jnp.bitwise_and(full, 1) == 1

            @pl.when(odd)
            def _():
                scores(last, s1, top1)
                absorb(last - 1, s0[...], top0[...])
                absorb_last(last, s1)

            @pl.when(jnp.logical_not(odd))
            def _():
                absorb_last(last, s0)

            out = acc_s[...] / sum_s[...]
            row_live = block * BLOCK + down < live
            for g in range(GROUP):
                piece = jnp.where(row_live, out[:, g * BLOCK : (g + 1) * BLOCK].T, 0.0)
                out_ref[0, :, g * LANES : (g + 1) * LANES] = piece.astype(jnp.bfloat16)

    for out_ref, k in zip(out_refs, shifts):
        one_block(out_ref, jnp.bitwise_xor(x, k))


def join_kernel(a_ref, b_ref, c_ref, d_ref, out_ref):
    x = lax.axis_index("x")
    for k, ref in enumerate((a_ref, b_ref, c_ref, d_ref)):
        head = jnp.bitwise_xor(x, k)
        col = pl.multiple_of(head * (GROUP * LANES), LANES)
        out_ref[0, :, pl.ds(col, GROUP * LANES)] = ref[0]


def vmem():
    return pl.BlockSpec(memory_space=pltpu.VMEM)


def smem():
    return pl.BlockSpec(memory_space=pltpu.SMEM)


def anywhere():
    return pl.BlockSpec(memory_space=pl.ANY)


def params(limit=VMEM_LIMIT):
    return pltpu.CompilerParams(vmem_limit_bytes=limit)


def exchange(value, axes):
    return lax.all_to_all(value, axes, split_axis=0, concat_axis=0, tiled=True)


def shift(value, axis, by):
    return lax.ppermute(value, axis, [(i, (i + by) % 4) for i in range(4)])


def swap(value, k):
    return lax.ppermute(value, "x", [(i, i ^ k) for i in range(4)])


def shift_upper(value, by):
    return lax.ppermute(value, ("zh", "y"), [(4 + i, 4 + (i + by) % 4) for i in range(4)])


def near(value):
    return pltpu.with_memory_space_constraint(value, pltpu.VMEM)


def local(q_frames, k_frames, v_frames, video_frames, frame_section, frame_offset):
    order = [pltpu.SMEM((16,), jnp.int32), pltpu.SMEM((8,), jnp.int32)]
    kv_send = pl.pallas_call(
        prep_kv_kernel,
        out_shape=jax.ShapeDtypeStruct((64, 32, LANES), jnp.bfloat16),
        in_specs=[smem(), vmem(), vmem()],
        out_specs=vmem(),
        scratch_shapes=order,
        compiler_params=params(VMEM_ALL),
        name="prep_kv",
    )(frame_section, k_frames, v_frames)
    q_send = pl.pallas_call(
        prep_q_kernel,
        out_shape=jax.ShapeDtypeStruct((32, GROUP * 16 + 8, LANES), jnp.bfloat16),
        in_specs=[smem(), smem(), vmem()],
        out_specs=vmem(),
        scratch_shapes=order,
        compiler_params=params(VMEM_ALL),
        name="prep_q",
    )(frame_section, frame_offset, q_frames)
    own = exchange(kv_send, ("zh", "x", "zl", "core"))
    q_send, own = lax.optimization_barrier((q_send, own))
    q_got = exchange(q_send, ("x", "zl", "core"))
    prev, nxt = shift(own, "y", 1), shift(own, "y", -1)
    pieces = [own, prev, nxt, shift(prev[:, :16], "y", 1), shift(nxt[:, 16:], "y", -1)]
    tiles = pl.pallas_call(
        arrange_kernel,
        out_shape=jax.ShapeDtypeStruct((8, 4, 8, 32, LANES), jnp.bfloat16),
        in_specs=[vmem()] * 5,
        out_specs=vmem(),
        compiler_params=params(),
        name="arrange",
    )(*[near(p) for p in pieces])
    tiles, q_got = near(tiles), near(q_got)

    def attend(shifts):
        rows = GROUP * BLOCK
        wide = pltpu.VMEM((TILE, rows), jnp.float32)
        top = pltpu.VMEM((8, rows), jnp.float32)
        line = pltpu.VMEM((1, rows), jnp.float32)
        return pl.pallas_call(
            functools.partial(attend_kernel, shifts),
            out_shape=[jax.ShapeDtypeStruct((1, BLOCK, rows), jnp.bfloat16)] * len(shifts),
            in_specs=[smem(), vmem(), vmem()],
            out_specs=[vmem()] * len(shifts),
            scratch_shapes=[
                pltpu.VMEM((LANES, rows), jnp.bfloat16),
                pltpu.VMEM((TILE, LANES), jnp.float32),
                wide,
                wide,
                top,
                top,
                line,
                line,
                pltpu.VMEM((LANES, rows), jnp.float32),
            ],
            compiler_params=params(),
            cost_estimate=pl.CostEstimate(
                flops=2 * 2 * rows * 4096 * LANES,
                transcendentals=rows * 4096,
                bytes_accessed=3 << 20,
            ),
            name="attend",
        )(video_frames, q_got, tiles)

    parts = {}
    for pair in ((1, 2), (3,), (0,)):
        blocks = attend(pair)
        for part, k in zip(blocks, pair):
            parts[k] = swap(part, k) if k else part
    return pl.pallas_call(
        join_kernel,
        out_shape=jax.ShapeDtypeStruct((1, BLOCK, HEADS_KV * GROUP * LANES), jnp.bfloat16),
        in_specs=[vmem()] * 4,
        out_specs=vmem(),
        compiler_params=params(),
        name="join",
    )(*[near(parts[k]) for k in range(4)])


def solution(mesh):
    fine = Mesh(mesh.devices.reshape(4, 2, 2, 4, 4), ("zl", "core", "zh", "x", "y"))
    ctx = ("zh", "x", "y")
    return jax.shard_map(
        local,
        mesh=fine,
        in_specs=(
            P(SEC, ctx, None, None),
            P(SEC, ctx, None, None),
            P(SEC, ctx, None, None),
            P(),
            P(SEC, ctx),
            P(SEC, ctx),
        ),
        out_specs=P(SEC, ctx, None),
        check_vma=False,
    )
```

time: 140 us -> 91.4 us (0.65)
  the two profiles are of different devices: /device:TPU:128 before, /device:TPU:198 now
where the time goes in v2:
time: 91.4 us; the launch traced here: 91 us
  waiting for transfers between devices  31.6 us (35%)
  starting transfers between devices  31 us (34%)
  Pallas kernels  28.3 us (31%)
    pallas_call x3, Pallas kernels, attend(): pl.pallas_call(functools.partial(attend_kernel, shifts), out_shape=[jax.S...  22.5 us
    ppermute x4, waiting for transfers between devices, shift(): return lax.ppermute(value, axis, [(i, (i + by) % 4) for i in range(4)])  19.9 us
    all_to_all x2, starting transfers between devices, exchange(): return lax.all_to_all(value, axes, split_axis=0, concat_axis=0, tiled=True)  17.3 us
    all_to_all x2, waiting for transfers between devices, exchange(): return lax.all_to_all(value, axes, split_axis=0, concat_axis=0, tiled=True)  11.6 us
    ppermute x4, starting transfers between devices, shift(): return lax.ppermute(value, axis, [(i, (i + by) % 4) for i in range(4)])  6.95 us
    ppermute x3, starting transfers between devices, swap(): return lax.ppermute(value, 'x', [(i, i ^ k) for i in range(4)])  6.77 us
    pallas_call x1, Pallas kernels, local(): pl.pallas_call(prep_q_kernel, out_shape=jax.ShapeDtypeStruct((32, GROUP *...  2.58 us
    pallas_call x1, Pallas kernels, local(): pl.pallas_call(prep_kv_kernel, out_shape=jax.ShapeDtypeStruct((64, 32, LA...  2.05 us
  transfers between devices with their start and end apart: 9, of which 4 were waited for; matrix products, arithmetic and copies ran while one was open for 0% of the time, Pallas kernels for 16%

profile of v2, /device:TPU:198, one launch (start us, length us, event | category | flops | bytes accessed | tf_op | source)
XLA Modules:
  0.0 91.0 jit_solution(7261330009170182972)
XLA Ops:
  0.0 2.1 %prep_kv.1 = bf16[64,32,128]{2,1,0:T(8,128)(2,1)} custom-call(s32[1,16]{1,0:T(1,128)} %sec_ref.3, bf16[1,16,8,512]{3,2,1,0:T(8,128)(2,1)} %k_ref.1, bf16[1,16,8,512]{3,2,1,0:T(8,128)(2,1)} %v_ref.1), custom_call_target="tpu_custom_call" | custom-call | tf_op jit(solution)/shard_map/prep_kv/pallas_call | solution.py:228
  2.1 9.5 %all-to-all-start = ((bf16[64,32,128]{2,1,0:T(8,128)(2,1)}), bf16[64,32,128]{2,1,0:T(8,128)(2,1)S(1)}, u32[]{:S(2)}, u32[]{:S(2)}) async-start(bf16[64,32,128]{2,1,0:T(8,128)(2,1)} %prep_kv.1), calls=%async_computation | async-start | bytes 1048576 | tf_op jit(solution)/shard_map/all_to_all | solution.py:207
  11.6 2.6 %prep_q.1 = bf16[32,120,128]{2,1,0:T(8,128)(2,1)} custom-call(s32[1,16]{1,0:T(1,128)} %sec_ref.3, s32[1,16]{1,0:T(1,128)} %off_ref.1, bf16[1,16,8,3584]{3,2,1,0:T(8,128)(2,1)} %q_ref.1), custom_call_target="tpu_custom_call" | custom-call | tf_op jit(solution)/shard_map/prep_q/pallas_call | solution.py:237
  14.2 11.6 %all-to-all-done.refs_0_ = bf16[64,32,128]{2,1,0:T(8,128)(2,1)S(1)} async-done(((bf16[64,32,128]{2,1,0:T(8,128)(2,1)}), bf16[64,32,128]{2,1,0:T(8,128)(2,1)S(1)}, u32[]{:S(2)}, u32[]{:S(2)}) %all-to-all-start) | async-done | bytes 524320 | tf_op jit(solution)/shard_map/all_to_all | solution.py:207
  25.8 7.8 %all-to-all-start.1 = ((bf16[32,120,128]{2,1,0:T(8,128)(2,1)}), bf16[32,120,128]{2,1,0:T(8,128)(2,1)}, u32[]{:S(2)}, u32[]{:S(2)}) async-start(bf16[32,120,128]{2,1,0:T(8,128)(2,1)} %prep_q.1), calls=%async_computation.1 | async-start | bytes 1966080 | tf_op jit(solution)/shard_map/all_to_all | solution.py:207
  33.5 3.1 %collective-permute-start.1 = (bf16[64,32,128]{2,1,0:T(8,128)(2,1)S(1)}, bf16[64,32,128]{2,1,0:T(8,128)(2,1)S(1)}, u32[]{:S(2)}, u32[]{:S(2)}) collective-permute-start(bf16[64,32,128]{2,1,0:T(8,128)(2,1)S(1)} %all-to-all-done.refs_0_), channel_id=1, source_target_pairs={{0,3},{1,0},{2,1},{3,2},{4,7},{5,4},{6,5},{7,6},{8,11},{9,8},{10,9... | collective-permute-start | bytes 1572872 | tf_op jit(solution)/shard_map/ppermute | solution.py:211
  36.6 0.0 collective-permute-start
  36.6 11.5 %collective-permute-done.1.refs_2_ = bf16[64,32,128]{2,1,0:T(8,128)(2,1)S(1)} collective-permute-done((bf16[64,32,128]{2,1,0:T(8,128)(2,1)S(1)}, bf16[64,32,128]{2,1,0:T(8,128)(2,1)S(1)}, u32[]{:S(2)}, u32[]{:S(2)}) %collective-permute-start.1) | collective-permute-done | bytes 524320 | tf_op jit(solution)/shard_map/ppermute | solution.py:211
  48.2 3.8 %collective-permute-start.3 = (bf16[64,16,128]{2,1,0:T(8,128)(2,1)S(1)}, bf16[64,16,128]{2,1,0:T(8,128)(2,1)S(1)}, u32[]{:S(2)}, u32[]{:S(2)}) collective-permute-start(bf16[64,16,128]{2,1,0:T(8,128)(2,1)S(1)} %slice.9), channel_id=1, source_target_pairs={{0,3},{1,0},{2,1},{3,2},{4,7},{5,4},{6,5},{7,6},{8,11},{9,8},{10,9... | collective-permute-start | bytes 786440 | tf_op jit(solution)/shard_map/ppermute | solution.py:211
  51.9 0.0 collective-permute-done.refs_1_
  52.0 0.0 copy-start
  52.0 0.1 collective-permute-start.2
  52.1 4.9 %collective-permute-done.3.refs_4_ = bf16[64,16,128]{2,1,0:T(8,128)(2,1)S(1)} collective-permute-done((bf16[64,16,128]{2,1,0:T(8,128)(2,1)S(1)}, bf16[64,16,128]{2,1,0:T(8,128)(2,1)S(1)}, u32[]{:S(2)}, u32[]{:S(2)}) %collective-permute-start.3) | collective-permute-done | bytes 262176 | tf_op jit(solution)/shard_map/ppermute | solution.py:211
  57.0 3.5 %collective-permute-done.2.refs_3_ = bf16[64,16,128]{2,1,0:T(8,128)(2,1)S(1)} collective-permute-done((bf16[64,16,128]{2,1,0:T(8,128)(2,1)S(1)}, bf16[64,16,128]{2,1,0:T(8,128)(2,1)S(1)}, u32[]{:S(2)}, u32[]{:S(2)}) %collective-permute-start.2) | collective-permute-done | bytes 262176 | tf_op jit(solution)/shard_map/ppermute | solution.py:211
  60.5 0.1 arrange.1.kv_ref
  60.6 0.0 all-to-all-done.1.q_ref
  60.7 0.0 copy-done
  60.7 10.6 %attend.4 = (bf16[1,128,896]{2,1,0:T(8,128)(2,1)S(1)}, bf16[1,128,896]{2,1,0:T(8,128)(2,1)S(1)}) custom-call(s32[8]{0:T(128)S(1)} %copy-done, bf16[32,120,128]{2,1,0:T(8,128)(2,1)} %all-to-all-done.1.q_ref, bf16[8,4,8,32,128]{4,3,2,1,0:T(8,128)(2,1)S(1)} %arrange.1.kv_ref), custom_call_target="tpu_custom_call" | custom-call | flops 1879048192 | bytes 3145728 | tf_op jit(solution)/shard_map/attend/pallas_call | solution.py:266
  71.3 1.2 %collective-permute-start.4 = (bf16[1,128,896]{2,1,0:T(8,128)(2,1)S(1)}, bf16[1,128,896]{2,1,0:T(8,128)(2,1)S(1)}, u32[]{:S(2)}, u32[]{:S(2)}) collective-permute-start(bf16[1,128,896]{2,1,0:T(8,128)(2,1)S(1)} %get-tuple-element.11), channel_id=1, source_target_pairs={{0,4},{4,0},{8,12},{12,8},{1,5},{5,1},{9,13},{13,9},{2,6},{6,2},{1... | collective-permute-start | bytes 688136 | tf_op jit(solution)/shard_map/ppermute | solution.py:215
  72.5 1.2 %collective-permute-start.5 = (bf16[1,128,896]{2,1,0:T(8,128)(2,1)S(1)}, bf16[1,128,896]{2,1,0:T(8,128)(2,1)S(1)}, u32[]{:S(2)}, u32[]{:S(2)}) collective-permute-start(bf16[1,128,896]{2,1,0:T(8,128)(2,1)S(1)} %get-tuple-element.12), channel_id=1, source_target_pairs={{0,8},{4,12},{8,0},{12,4},{1,9},{5,13},{9,1},{13,5},{2,10},{6,14},... | collective-permute-start | bytes 688136 | tf_op jit(solution)/shard_map/ppermute | solution.py:215
  73.6 5.1 %attend.5 = bf16[1,128,896]{2,1,0:T(8,128)(2,1)S(1)} custom-call(s32[8]{0:T(128)S(1)} %copy-done, bf16[32,120,128]{2,1,0:T(8,128)(2,1)} %all-to-all-done.1.q_ref, bf16[8,4,8,32,128]{4,3,2,1,0:T(8,128)(2,1)S(1)} %arrange.1.kv_ref), custom_call_target="tpu_custom_call" | custom-call | flops 1879048192 | bytes 3145728 | tf_op jit(solution)/shard_map/attend/pallas_call | solution.py:266
  78.7 4.4 %collective-permute-start.6 = (bf16[1,128,896]{2,1,0:T(8,128)(2,1)S(1)}, bf16[1,128,896]{2,1,0:T(8,128)(2,1)S(1)}, u32[]{:S(2)}, u32[]{:S(2)}) collective-permute-start(bf16[1,128,896]{2,1,0:T(8,128)(2,1)S(1)} %attend.5), channel_id=1, source_target_pairs={{0,12},{4,8},{8,4},{12,0},{1,13},{5,9},{9,5},{13,1},{2,14},{6,10},... | collective-permute-start | bytes 688136 | tf_op jit(solution)/shard_map/ppermute | solution.py:215
  83.1 6.8 %attend.3.a_ref = bf16[1,128,896]{2,1,0:T(8,128)(2,1)S(1)} custom-call(s32[8]{0:T(128)S(1)} %copy-done, bf16[32,120,128]{2,1,0:T(8,128)(2,1)} %all-to-all-done.1.q_ref, bf16[8,4,8,32,128]{4,3,2,1,0:T(8,128)(2,1)S(1)} %arrange.1.kv_ref), custom_call_target="tpu_custom_call" | custom-call | flops 1879048192 | bytes 3145728 | tf_op jit(solution)/shard_map/attend/pallas_call | solution.py:266
  89.9 0.0 collective-permute-done.4.b_ref
  90.0 0.0 collective-permute-done.5.c_ref
  90.0 0.0 collective-permute-done.6.d_ref
  90.0 1.0 %join.1 = bf16[1,128,3584]{2,1,0:T(8,128)(2,1)} custom-call(bf16[1,128,896]{2,1,0:T(8,128)(2,1)S(1)} %attend.3.a_ref, bf16[1,128,896]{2,1,0:T(8,128)(2,1)S(1)} %collective-permute-done.4.b_ref, bf16[1,128,896]{2,1,0:T(8,128)(2,1)S(1)} %collective-permute-done.5.c_ref, bf16[1,128,896]{2,1,0:T(8,128)(2,1)S(1)} %collective-permute-done.6.d_ref), custom_call_target="tpu_custom_call" | custom-call | tf_op jit(solution)/shard_map/join/pallas_call | solution.py:296
  (2 shorter events, 0.0 us)
Async XLA Ops:
  2.1 23.7 %all-to-all-start = ((bf16[64,32,128]{2,1,0:T(8,128)(2,1)}), bf16[64,32,128]{2,1,0:T(8,128)(2,1)S(1)}, u32[]{:S(2)}, u32[]{:S(2)}) async-start(bf16[64,32,128]{2,1,0:T(8,128)(2,1)} %prep_kv.1), calls=%async_computation | async-start | bytes 1048576 | tf_op jit(solution)/shard_map/all_to_all | solution.py:207
  25.8 34.9 %all-to-all-start.1 = ((bf16[32,120,128]{2,1,0:T(8,128)(2,1)}), bf16[32,120,128]{2,1,0:T(8,128)(2,1)}, u32[]{:S(2)}, u32[]{:S(2)}) async-start(bf16[32,120,128]{2,1,0:T(8,128)(2,1)} %prep_q.1), calls=%async_computation.1 | async-start | bytes 1966080 | tf_op jit(solution)/shard_map/all_to_all | solution.py:207
  33.5 14.6 %collective-permute-start.1 = (bf16[64,32,128]{2,1,0:T(8,128)(2,1)S(1)}, bf16[64,32,128]{2,1,0:T(8,128)(2,1)S(1)}, u32[]{:S(2)}, u32[]{:S(2)}) collective-permute-start(bf16[64,32,128]{2,1,0:T(8,128)(2,1)S(1)} %all-to-all-done.refs_0_), channel_id=1, source_target_pairs={{0,3},{1,0},{2,1},{3,2},{4,7},{5,4},{6,5},{7,6},{8,11},{9,8},{10,9... | collective-permute-start | bytes 1572872 | tf_op jit(solution)/shard_map/ppermute | solution.py:211
  36.6 15.3 %collective-permute-start = (bf16[64,32,128]{2,1,0:T(8,128)(2,1)S(1)}, bf16[64,32,128]{2,1,0:T(8,128)(2,1)S(1)}, u32[]{:S(2)}, u32[]{:S(2)}) collective-permute-start(bf16[64,32,128]{2,1,0:T(8,128)(2,1)S(1)} %all-to-all-done.refs_0_), channel_id=1, source_target_pairs={{0,1},{1,2},{2,3},{3,0},{4,5},{5,6},{6,7},{7,4},{8,9},{9,10},{10,1... | collective-permute-start | bytes 1572872 | tf_op jit(solution)/shard_map/ppermute | solution.py:211
  48.2 8.8 %collective-permute-start.3 = (bf16[64,16,128]{2,1,0:T(8,128)(2,1)S(1)}, bf16[64,16,128]{2,1,0:T(8,128)(2,1)S(1)}, u32[]{:S(2)}, u32[]{:S(2)}) collective-permute-start(bf16[64,16,128]{2,1,0:T(8,128)(2,1)S(1)} %slice.9), channel_id=1, source_target_pairs={{0,3},{1,0},{2,1},{3,2},{4,7},{5,4},{6,5},{7,6},{8,11},{9,8},{10,9... | collective-permute-start | bytes 786440 | tf_op jit(solution)/shard_map/ppermute | solution.py:211
  52.0 8.7 %copy-start = (s32[8]{0:T(128)S(1)}, s32[8]{0:T(128)}, u32[]{:S(2)}) copy-start(s32[8]{0:T(128)} %video_ref.5) | copy-start | bytes 100
  52.0 8.5 %collective-permute-start.2 = (bf16[64,16,128]{2,1,0:T(8,128)(2,1)S(1)}, bf16[64,16,128]{2,1,0:T(8,128)(2,1)S(1)}, u32[]{:S(2)}, u32[]{:S(2)}) collective-permute-start(bf16[64,16,128]{2,1,0:T(8,128)(2,1)S(1)} %slice.8), channel_id=1, source_target_pairs={{0,1},{1,2},{2,3},{3,0},{4,5},{5,6},{6,7},{7,4},{8,9},{9,10},{10,1... | collective-permute-start | bytes 786440 | tf_op jit(solution)/shard_map/ppermute | solution.py:211
  71.3 18.7 %collective-permute-start.4 = (bf16[1,128,896]{2,1,0:T(8,128)(2,1)S(1)}, bf16[1,128,896]{2,1,0:T(8,128)(2,1)S(1)}, u32[]{:S(2)}, u32[]{:S(2)}) collective-permute-start(bf16[1,128,896]{2,1,0:T(8,128)(2,1)S(1)} %get-tuple-element.11), channel_id=1, source_target_pairs={{0,4},{4,0},{8,12},{12,8},{1,5},{5,1},{9,13},{13,9},{2,6},{6,2},{1... | collective-permute-start | bytes 688136 | tf_op jit(solution)/shard_map/ppermute | solution.py:215
  72.5 17.5 %collective-permute-start.5 = (bf16[1,128,896]{2,1,0:T(8,128)(2,1)S(1)}, bf16[1,128,896]{2,1,0:T(8,128)(2,1)S(1)}, u32[]{:S(2)}, u32[]{:S(2)}) collective-permute-start(bf16[1,128,896]{2,1,0:T(8,128)(2,1)S(1)} %get-tuple-element.12), channel_id=1, source_target_pairs={{0,8},{4,12},{8,0},{12,4},{1,9},{5,13},{9,1},{13,5},{2,10},{6,14},... | collective-permute-start | bytes 688136 | tf_op jit(solution)/shard_map/ppermute | solution.py:215
  78.7 11.3 %collective-permute-start.6 = (bf16[1,128,896]{2,1,0:T(8,128)(2,1)S(1)}, bf16[1,128,896]{2,1,0:T(8,128)(2,1)S(1)}, u32[]{:S(2)}, u32[]{:S(2)}) collective-permute-start(bf16[1,128,896]{2,1,0:T(8,128)(2,1)S(1)} %attend.5), channel_id=1, source_target_pairs={{0,12},{4,8},{8,4},{12,0},{1,13},{5,9},{9,5},{13,1},{2,14},{6,10},... | collective-permute-start | bytes 688136 | tf_op jit(solution)/shard_map/ppermute | solution.py:215

commit v3 on v2

--- a/solution.py
+++ b/solution.py
@@ -89,7 +89,6 @@
     rows = GROUP * BLOCK
     factor = math.log2(math.e) / math.sqrt(128.0)
     down = lax.broadcasted_iota(jnp.int32, (BLOCK, LANES), 0)
-    across = lax.broadcasted_iota(jnp.int32, (BLOCK, LANES), 1)
 
     def dot(a, b, ca, cb):
         return lax.dot_general(
@@ -129,13 +128,14 @@
             last = zh * 4 + xb
             meta = q_ref[pl.ds(xb * 8, 8), GROUP * 16 :, :].astype(jnp.float32)
             pos = jnp.sum(meta, axis=0)[0:1]
-            pick = (down.astype(jnp.float32) == pos).astype(jnp.float32).astype(jnp.bfloat16)
             for g in range(GROUP):
-                raw = q_ref[pl.ds(xb * 8, 8), g * 16 : (g + 1) * 16, :].reshape(BLOCK, LANES)
-                q_s[:, g * BLOCK : (g + 1) * BLOCK] = dot(raw, pick, 0, 1).astype(jnp.bfloat16)
-            reach = (down <= across) & (block * BLOCK + down < live)
-            seen = dot(pick, reach.astype(jnp.float32).astype(jnp.bfloat16), 0, 0)
-            mask_s[0:BLOCK, :] = jnp.where(seen > 0.5, 0.0, NEG)
+                raw = q_ref[pl.ds(xb * 8, 8), g * 16 : (g + 1) * 16, :]
+                q_s[:, g * BLOCK : (g + 1) * BLOCK] = raw.reshape(BLOCK, LANES).T
+            query_pos = jnp.broadcast_to(pos, (BLOCK, LANES))
+            key_pos = query_pos.T
+            live_rows = (live - block * BLOCK).astype(jnp.float32)
+            reach = (key_pos <= query_pos) & (key_pos < live_rows)
+            mask_s[0:BLOCK, :] = jnp.where(reach, 0.0, NEG)
             for a, by in ((1, 3), (2, 1), (3, 2)):
                 before = jnp.bitwise_and(y + by, 3) < y
                 mask_s[a * BLOCK : (a + 1) * BLOCK, :] = jnp.full(
@@ -145,38 +145,73 @@
             sum_s[...] = jnp.zeros((1, rows), jnp.float32)
             acc_s[...] = jnp.zeros((LANES, rows), jnp.float32)
 
-            scores(first, s0, top0)
-            full = last - first
-
-            def pair(n, _):
-                t = first + 2 * n
-                scores(t + 1, s1, top1)
-                absorb(t, s0[...], top0[...])
-                scores(t + 2, s0, top0)
-                absorb(t + 1, s1[...], top1[...])
-                return 0
-
-            lax.fori_loop(0, lax.shift_right_logical(full, 1), pair, 0)
-            odd = jnp.bitwise_and(full, 1) == 1
-
-            @pl.when(odd)
-            def _():
-                scores(last, s1, top1)
-                absorb(last - 1, s0[...], top0[...])
-                absorb_last(last, s1)
-
-            @pl.when(jnp.logical_not(odd))
-            def _():
-                absorb_last(last, s0)
-
-            out = acc_s[...] / sum_s[...]
-            row_live = block * BLOCK + down < live
+            if len(shifts) > 1:
+                bufs = ((s0, top0), (s1, top1))
+                scores(first, s0, top0)
+
+                @pl.when(zh == 1)
+                def _():
+                    for t in range(4):
+                        scores(t + 1, *bufs[(t + 1) % 2])
+                        absorb(t, bufs[t % 2][0][...], bufs[t % 2][1][...])
+
+                own = zh * 4
+                for n in range(4):
+
+                    @pl.when(xb == n)
+                    def _():
+                        for t in range(n):
+                            scores(own + t + 1, *bufs[(t + 1) % 2])
+                            absorb(own + t, bufs[t % 2][0][...], bufs[t % 2][1][...])
+                        absorb_last(last, bufs[n % 2][0])
+
+            else:
+                scores(first, s0, top0)
+                full = last - first
+
+                def pair(n, _):
+                    t = first + 2 * n
+                    scores(t + 1, s1, top1)
+                    absorb(t, s0[...], top0[...])
+                    scores(t + 2, s0, top0)
+                    absorb(t + 1, s1[...], top1[...])
+                    return 0
+
+                lax.fori_loop(0, lax.shift_right_logical(full, 1), pair, 0)
+                odd = jnp.bitwise_and(full, 1) == 1
+
+                @pl.when(odd)
+                def _():
+                    scores(last, s1, top1)
+                    absorb(last - 1, s0[...], top0[...])
+                    absorb_last(last, s1)
+
+                @pl.when(jnp.logical_not(odd))
+                def _():
+                    absorb_last(last, s0)
+
+            pick = (down.astype(jnp.float32) == pos).astype(jnp.float32).astype(jnp.bfloat16)
+            scale = 1.0 / sum_s[...]
             for g in range(GROUP):
-                piece = jnp.where(row_live, out[:, g * BLOCK : (g + 1) * BLOCK].T, 0.0)
-                out_ref[0, :, g * LANES : (g + 1) * LANES] = piece.astype(jnp.bfloat16)
+                at = slice(g * BLOCK, (g + 1) * BLOCK)
+                piece = jnp.where(pos < live_rows, acc_s[:, at] * scale[:, at], 0.0)
+                out_ref[0, :, g * LANES : (g + 1) * LANES] = dot(
+                    pick, piece.astype(jnp.bfloat16), 1, 1
+                ).astype(jnp.bfloat16)
 
     for out_ref, k in zip(out_refs, shifts):
         one_block(out_ref, jnp.bitwise_xor(x, k))
+
+
+def attend_scratch():
+    rows = GROUP * BLOCK
+    wide = pltpu.VMEM((TILE, rows), jnp.float32)
+    top = pltpu.VMEM((8, rows), jnp.float32)
+    line = pltpu.VMEM((1, rows), jnp.float32)
+    queries = pltpu.VMEM((LANES, rows), jnp.bfloat16)
+    mask = pltpu.VMEM((TILE, LANES), jnp.float32)
+    total = pltpu.VMEM((LANES, rows), jnp.float32)
+    return [queries, mask, wide, wide, top, top, line, line, total]
 
 
 def join_kernel(a_ref, b_ref, c_ref, d_ref, out_ref):
@@ -260,25 +295,12 @@
 
     def attend(shifts):
         rows = GROUP * BLOCK
-        wide = pltpu.VMEM((TILE, rows), jnp.float32)
-        top = pltpu.VMEM((8, rows), jnp.float32)
-        line = pltpu.VMEM((1, rows), jnp.float32)
         return pl.pallas_call(
             functools.partial(attend_kernel, shifts),
             out_shape=[jax.ShapeDtypeStruct((1, BLOCK, rows), jnp.bfloat16)] * len(shifts),
             in_specs=[smem(), vmem(), vmem()],
             out_specs=[vmem()] * len(shifts),
-            scratch_shapes=[
-                pltpu.VMEM((LANES, rows), jnp.bfloat16),
-                pltpu.VMEM((TILE, LANES), jnp.float32),
-                wide,
-                wide,
-                top,
-                top,
-                line,
-                line,
-                pltpu.VMEM((LANES, rows), jnp.float32),
-            ],
+            scratch_shapes=attend_scratch(),
             compiler_params=params(),
             cost_estimate=pl.CostEstimate(
                 flops=2 * 2 * rows * 4096 * LANES,

time: 91.4 us -> 90.4 us (0.989)
  the two profiles are of different devices: /device:TPU:198 before, /device:TPU:128 now
where the time goes in v3:
time: 90.4 us; the launch traced here: 89.7 us
  waiting for transfers between devices  34.6 us (38%)
  Pallas kernels  27.9 us (31%)
  starting transfers between devices  27.1 us (30%)
    pallas_call x3, Pallas kernels, attend(): pl.pallas_call(functools.partial(attend_kernel, shifts), out_shape=[jax.S...  22.1 us
    ppermute x4, waiting for transfers between devices, shift(): return lax.ppermute(value, axis, [(i, (i + by) % 4) for i in range(4)])  20.2 us
    all_to_all x2, starting transfers between devices, exchange(): return lax.all_to_all(value, axes, split_axis=0, concat_axis=0, tiled=True)  15.5 us
    all_to_all x2, waiting for transfers between devices, exchange(): return lax.all_to_all(value, axes, split_axis=0, concat_axis=0, tiled=True)  12.3 us
    ppermute x4, starting transfers between devices, shift(): return lax.ppermute(value, axis, [(i, (i + by) % 4) for i in range(4)])  6.95 us
    ppermute x3, starting transfers between devices, swap(): return lax.ppermute(value, 'x', [(i, i ^ k) for i in range(4)])  4.7 us
    pallas_call x1, Pallas kernels, local(): pl.pallas_call(prep_q_kernel, out_shape=jax.ShapeDtypeStruct((32, GROUP *...  2.58 us
    ppermute x3, waiting for transfers between devices, swap(): return lax.ppermute(value, 'x', [(i, i ^ k) for i in range(4)])  2.11 us
  transfers between devices with their start and end apart: 9, of which 5 were waited for; matrix products, arithmetic and copies ran while one was open for 0% of the time, Pallas kernels for 16%

profile of v3, /device:TPU:128, one launch (start us, length us, event | category | flops | bytes accessed | tf_op | source)
XLA Modules:
  0.0 89.7 jit_solution(10259916216126652104)
XLA Ops:
  0.0 2.1 %prep_kv.1 = bf16[64,32,128]{2,1,0:T(8,128)(2,1)} custom-call(s32[1,16]{1,0:T(1,128)} %sec_ref.3, bf16[1,16,8,512]{3,2,1,0:T(8,128)(2,1)} %k_ref.1, bf16[1,16,8,512]{3,2,1,0:T(8,128)(2,1)} %v_ref.1), custom_call_target="tpu_custom_call" | custom-call | tf_op jit(solution)/shard_map/prep_kv/pallas_call | solution.py:263
  2.1 10.3 %all-to-all-start = ((bf16[64,32,128]{2,1,0:T(8,128)(2,1)}), bf16[64,32,128]{2,1,0:T(8,128)(2,1)S(1)}, u32[]{:S(2)}, u32[]{:S(2)}) async-start(bf16[64,32,128]{2,1,0:T(8,128)(2,1)} %prep_kv.1), calls=%async_computation | async-start | bytes 1048576 | tf_op jit(solution)/shard_map/all_to_all | solution.py:242
  12.4 2.6 %prep_q.1 = bf16[32,120,128]{2,1,0:T(8,128)(2,1)} custom-call(s32[1,16]{1,0:T(1,128)} %sec_ref.3, s32[1,16]{1,0:T(1,128)} %off_ref.1, bf16[1,16,8,3584]{3,2,1,0:T(8,128)(2,1)} %q_ref.1), custom_call_target="tpu_custom_call" | custom-call | tf_op jit(solution)/shard_map/prep_q/pallas_call | solution.py:272
  15.0 12.3 %all-to-all-done.refs_0_ = bf16[64,32,128]{2,1,0:T(8,128)(2,1)S(1)} async-done(((bf16[64,32,128]{2,1,0:T(8,128)(2,1)}), bf16[64,32,128]{2,1,0:T(8,128)(2,1)S(1)}, u32[]{:S(2)}, u32[]{:S(2)}) %all-to-all-start) | async-done | bytes 524320 | tf_op jit(solution)/shard_map/all_to_all | solution.py:242
  27.3 5.1 %all-to-all-start.1 = ((bf16[32,120,128]{2,1,0:T(8,128)(2,1)}), bf16[32,120,128]{2,1,0:T(8,128)(2,1)}, u32[]{:S(2)}, u32[]{:S(2)}) async-start(bf16[32,120,128]{2,1,0:T(8,128)(2,1)} %prep_q.1), calls=%async_computation.1 | async-start | bytes 1966080 | tf_op jit(solution)/shard_map/all_to_all | solution.py:242
  32.4 3.1 %collective-permute-start.1 = (bf16[64,32,128]{2,1,0:T(8,128)(2,1)S(1)}, bf16[64,32,128]{2,1,0:T(8,128)(2,1)S(1)}, u32[]{:S(2)}, u32[]{:S(2)}) collective-permute-start(bf16[64,32,128]{2,1,0:T(8,128)(2,1)S(1)} %all-to-all-done.refs_0_), channel_id=1, source_target_pairs={{0,3},{1,0},{2,1},{3,2},{4,7},{5,4},{6,5},{7,6},{8,11},{9,8},{10,9... | collective-permute-start | bytes 1572872 | tf_op jit(solution)/shard_map/ppermute | solution.py:246
  35.5 0.0 collective-permute-start
  35.5 11.6 %collective-permute-done.1.refs_2_ = bf16[64,32,128]{2,1,0:T(8,128)(2,1)S(1)} collective-permute-done((bf16[64,32,128]{2,1,0:T(8,128)(2,1)S(1)}, bf16[64,32,128]{2,1,0:T(8,128)(2,1)S(1)}, u32[]{:S(2)}, u32[]{:S(2)}) %collective-permute-start.1) | collective-permute-done | bytes 524320 | tf_op jit(solution)/shard_map/ppermute | solution.py:246
  47.1 3.8 %collective-permute-start.3 = (bf16[64,16,128]{2,1,0:T(8,128)(2,1)S(1)}, bf16[64,16,128]{2,1,0:T(8,128)(2,1)S(1)}, u32[]{:S(2)}, u32[]{:S(2)}) collective-permute-start(bf16[64,16,128]{2,1,0:T(8,128)(2,1)S(1)} %slice.9), channel_id=1, source_target_pairs={{0,3},{1,0},{2,1},{3,2},{4,7},{5,4},{6,5},{7,6},{8,11},{9,8},{10,9... | collective-permute-start | bytes 786440 | tf_op jit(solution)/shard_map/ppermute | solution.py:246
  50.8 0.0 collective-permute-done.refs_1_
  50.9 0.0 copy-start
  50.9 0.1 collective-permute-start.2
  51.0 5.1 %collective-permute-done.3.refs_4_ = bf16[64,16,128]{2,1,0:T(8,128)(2,1)S(1)} collective-permute-done((bf16[64,16,128]{2,1,0:T(8,128)(2,1)S(1)}, bf16[64,16,128]{2,1,0:T(8,128)(2,1)S(1)}, u32[]{:S(2)}, u32[]{:S(2)}) %collective-permute-start.3) | collective-permute-done | bytes 262176 | tf_op jit(solution)/shard_map/ppermute | solution.py:246
  56.1 3.5 %collective-permute-done.2.refs_3_ = bf16[64,16,128]{2,1,0:T(8,128)(2,1)S(1)} collective-permute-done((bf16[64,16,128]{2,1,0:T(8,128)(2,1)S(1)}, bf16[64,16,128]{2,1,0:T(8,128)(2,1)S(1)}, u32[]{:S(2)}, u32[]{:S(2)}) %collective-permute-start.2) | collective-permute-done | bytes 262176 | tf_op jit(solution)/shard_map/ppermute | solution.py:246
  59.6 0.1 arrange.1.kv_ref
  59.7 0.0 all-to-all-done.1.q_ref
  59.8 0.0 copy-done
  59.8 10.2 %attend.4 = (bf16[1,128,896]{2,1,0:T(8,128)(2,1)S(1)}, bf16[1,128,896]{2,1,0:T(8,128)(2,1)S(1)}) custom-call(s32[8]{0:T(128)S(1)} %copy-done, bf16[32,120,128]{2,1,0:T(8,128)(2,1)} %all-to-all-done.1.q_ref, bf16[8,4,8,32,128]{4,3,2,1,0:T(8,128)(2,1)S(1)} %arrange.1.kv_ref), custom_call_target="tpu_custom_call" | custom-call | flops 1879048192 | bytes 3145728 | tf_op jit(solution)/shard_map/attend/pallas_call | solution.py:298
  70.0 1.6 %collective-permute-start.4 = (bf16[1,128,896]{2,1,0:T(8,128)(2,1)S(1)}, bf16[1,128,896]{2,1,0:T(8,128)(2,1)S(1)}, u32[]{:S(2)}, u32[]{:S(2)}) collective-permute-start(bf16[1,128,896]{2,1,0:T(8,128)(2,1)S(1)} %get-tuple-element.11), channel_id=1, source_target_pairs={{0,4},{4,0},{8,12},{12,8},{1,5},{5,1},{9,13},{13,9},{2,6},{6,2},{1... | collective-permute-start | bytes 688136 | tf_op jit(solution)/shard_map/ppermute | solution.py:250
  71.6 2.8 %collective-permute-start.5 = (bf16[1,128,896]{2,1,0:T(8,128)(2,1)S(1)}, bf16[1,128,896]{2,1,0:T(8,128)(2,1)S(1)}, u32[]{:S(2)}, u32[]{:S(2)}) collective-permute-start(bf16[1,128,896]{2,1,0:T(8,128)(2,1)S(1)} %get-tuple-element.12), channel_id=1, source_target_pairs={{0,8},{4,12},{8,0},{12,4},{1,9},{5,13},{9,1},{13,5},{2,10},{6,14},... | collective-permute-start | bytes 688136 | tf_op jit(solution)/shard_map/ppermute | solution.py:250
  74.4 6.8 %attend.5 = bf16[1,128,896]{2,1,0:T(8,128)(2,1)S(1)} custom-call(s32[8]{0:T(128)S(1)} %copy-done, bf16[32,120,128]{2,1,0:T(8,128)(2,1)} %all-to-all-done.1.q_ref, bf16[8,4,8,32,128]{4,3,2,1,0:T(8,128)(2,1)S(1)} %arrange.1.kv_ref), custom_call_target="tpu_custom_call" | custom-call | flops 1879048192 | bytes 3145728 | tf_op jit(solution)/shard_map/attend/pallas_call | solution.py:298
  81.2 0.3 collective-permute-start.6
  81.5 5.1 %attend.3.a_ref = bf16[1,128,896]{2,1,0:T(8,128)(2,1)S(1)} custom-call(s32[8]{0:T(128)S(1)} %copy-done, bf16[32,120,128]{2,1,0:T(8,128)(2,1)} %all-to-all-done.1.q_ref, bf16[8,4,8,32,128]{4,3,2,1,0:T(8,128)(2,1)S(1)} %arrange.1.kv_ref), custom_call_target="tpu_custom_call" | custom-call | flops 1879048192 | bytes 3145728 | tf_op jit(solution)/shard_map/attend/pallas_call | solution.py:298
  86.6 0.0 collective-permute-done.4.b_ref
  86.6 0.0 collective-permute-done.5.c_ref
  86.6 2.1 %collective-permute-done.6.d_ref = bf16[1,128,896]{2,1,0:T(8,128)(2,1)S(1)} collective-permute-done((bf16[1,128,896]{2,1,0:T(8,128)(2,1)S(1)}, bf16[1,128,896]{2,1,0:T(8,128)(2,1)S(1)}, u32[]{:S(2)}, u32[]{:S(2)}) %collective-permute-start.6) | collective-permute-done | bytes 229408 | tf_op jit(solution)/shard_map/ppermute | solution.py:250
  88.7 1.0 %join.1 = bf16[1,128,3584]{2,1,0:T(8,128)(2,1)} custom-call(bf16[1,128,896]{2,1,0:T(8,128)(2,1)S(1)} %attend.3.a_ref, bf16[1,128,896]{2,1,0:T(8,128)(2,1)S(1)} %collective-permute-done.4.b_ref, bf16[1,128,896]{2,1,0:T(8,128)(2,1)S(1)} %collective-permute-done.5.c_ref, bf16[1,128,896]{2,1,0:T(8,128)(2,1)S(1)} %collective-permute-done.6.d_ref), custom_call_target="tpu_custom_call" | custom-call | tf_op jit(solution)/shard_map/join/pallas_call | solution.py:318
  (2 shorter events, 0.0 us)
Async XLA Ops:
  2.1 25.2 %all-to-all-start = ((bf16[64,32,128]{2,1,0:T(8,128)(2,1)}), bf16[64,32,128]{2,1,0:T(8,128)(2,1)S(1)}, u32[]{:S(2)}, u32[]{:S(2)}) async-start(bf16[64,32,128]{2,1,0:T(8,128)(2,1)} %prep_kv.1), calls=%async_computation | async-start | bytes 1048576 | tf_op jit(solution)/shard_map/all_to_all | solution.py:242
  27.3 32.5 %all-to-all-start.1 = ((bf16[32,120,128]{2,1,0:T(8,128)(2,1)}), bf16[32,120,128]{2,1,0:T(8,128)(2,1)}, u32[]{:S(2)}, u32[]{:S(2)}) async-start(bf16[32,120,128]{2,1,0:T(8,128)(2,1)} %prep_q.1), calls=%async_computation.1 | async-start | bytes 1966080 | tf_op jit(solution)/shard_map/all_to_all | solution.py:242
  32.4 14.6 %collective-permute-start.1 = (bf16[64,32,128]{2,1,0:T(8,128)(2,1)S(1)}, bf16[64,32,128]{2,1,0:T(8,128)(2,1)S(1)}, u32[]{:S(2)}, u32[]{:S(2)}) collective-permute-start(bf16[64,32,128]{2,1,0:T(8,128)(2,1)S(1)} %all-to-all-done.refs_0_), channel_id=1, source_target_pairs={{0,3},{1,0},{2,1},{3,2},{4,7},{5,4},{6,5},{7,6},{8,11},{9,8},{10,9... | collective-permute-start | bytes 1572872 | tf_op jit(solution)/shard_map/ppermute | solution.py:246
  35.5 15.3 %collective-permute-start = (bf16[64,32,128]{2,1,0:T(8,128)(2,1)S(1)}, bf16[64,32,128]{2,1,0:T(8,128)(2,1)S(1)}, u32[]{:S(2)}, u32[]{:S(2)}) collective-permute-start(bf16[64,32,128]{2,1,0:T(8,128)(2,1)S(1)} %all-to-all-done.refs_0_), channel_id=1, source_target_pairs={{0,1},{1,2},{2,3},{3,0},{4,5},{5,6},{6,7},{7,4},{8,9},{9,10},{10,1... | collective-permute-start | bytes 1572872 | tf_op jit(solution)/shard_map/ppermute | solution.py:246
  47.1 9.0 %collective-permute-start.3 = (bf16[64,16,128]{2,1,0:T(8,128)(2,1)S(1)}, bf16[64,16,128]{2,1,0:T(8,128)(2,1)S(1)}, u32[]{:S(2)}, u32[]{:S(2)}) collective-permute-start(bf16[64,16,128]{2,1,0:T(8,128)(2,1)S(1)} %slice.9), channel_id=1, source_target_pairs={{0,3},{1,0},{2,1},{3,2},{4,7},{5,4},{6,5},{7,6},{8,11},{9,8},{10,9... | collective-permute-start | bytes 786440 | tf_op jit(solution)/shard_map/ppermute | solution.py:246
  50.9 8.9 %copy-start = (s32[8]{0:T(128)S(1)}, s32[8]{0:T(128)}, u32[]{:S(2)}) copy-start(s32[8]{0:T(128)} %video_ref.5) | copy-start | bytes 100
  50.9 8.7 %collective-permute-start.2 = (bf16[64,16,128]{2,1,0:T(8,128)(2,1)S(1)}, bf16[64,16,128]{2,1,0:T(8,128)(2,1)S(1)}, u32[]{:S(2)}, u32[]{:S(2)}) collective-permute-start(bf16[64,16,128]{2,1,0:T(8,128)(2,1)S(1)} %slice.8), channel_id=1, source_target_pairs={{0,1},{1,2},{2,3},{3,0},{4,5},{5,6},{6,7},{7,4},{8,9},{9,10},{10,1... | collective-permute-start | bytes 786440 | tf_op jit(solution)/shard_map/ppermute | solution.py:246
  70.0 16.6 %collective-permute-start.4 = (bf16[1,128,896]{2,1,0:T(8,128)(2,1)S(1)}, bf16[1,128,896]{2,1,0:T(8,128)(2,1)S(1)}, u32[]{:S(2)}, u32[]{:S(2)}) collective-permute-start(bf16[1,128,896]{2,1,0:T(8,128)(2,1)S(1)} %get-tuple-element.11), channel_id=1, source_target_pairs={{0,4},{4,0},{8,12},{12,8},{1,5},{5,1},{9,13},{13,9},{2,6},{6,2},{1... | collective-permute-start | bytes 688136 | tf_op jit(solution)/shard_map/ppermute | solution.py:250
  71.6 15.0 %collective-permute-start.5 = (bf16[1,128,896]{2,1,0:T(8,128)(2,1)S(1)}, bf16[1,128,896]{2,1,0:T(8,128)(2,1)S(1)}, u32[]{:S(2)}, u32[]{:S(2)}) collective-permute-start(bf16[1,128,896]{2,1,0:T(8,128)(2,1)S(1)} %get-tuple-element.12), channel_id=1, source_target_pairs={{0,8},{4,12},{8,0},{12,4},{1,9},{5,13},{9,1},{13,5},{2,10},{6,14},... | collective-permute-start | bytes 688136 | tf_op jit(solution)/shard_map/ppermute | solution.py:250
  81.2 7.5 %collective-permute-start.6 = (bf16[1,128,896]{2,1,0:T(8,128)(2,1)S(1)}, bf16[1,128,896]{2,1,0:T(8,128)(2,1)S(1)}, u32[]{:S(2)}, u32[]{:S(2)}) collective-permute-start(bf16[1,128,896]{2,1,0:T(8,128)(2,1)S(1)} %attend.5), channel_id=1, source_target_pairs={{0,12},{4,8},{8,4},{12,0},{1,13},{5,9},{9,5},{13,1},{2,14},{6,10},... | collective-permute-start | bytes 688136 | tf_op jit(solution)/shard_map/ppermute | solution.py:250

commit v4 on v2

--- a/solution.py
+++ b/solution.py
@@ -82,14 +82,13 @@
     shifts, video_ref, q_ref, kv_ref, *refs
 ):
     out_refs = refs[: len(shifts)]
-    q_s, mask_s, s0, s1, top0, top1, max_s, sum_s, acc_s = refs[len(shifts) :]
+    q_s, mask_s, s0, s1, top0, top1, max_s, acc_s = refs[len(shifts) :]
     x, y, zh = lax.axis_index("x"), lax.axis_index("y"), lax.axis_index("zh")
     me = lax.axis_index("zl") * 2 + lax.axis_index("core")
     live = video_ref[me] * 8
     rows = GROUP * BLOCK
     factor = math.log2(math.e) / math.sqrt(128.0)
     down = lax.broadcasted_iota(jnp.int32, (BLOCK, LANES), 0)
-    across = lax.broadcasted_iota(jnp.int32, (BLOCK, LANES), 1)
 
     def dot(a, b, ca, cb):
         return lax.dot_general(
@@ -107,9 +106,10 @@
         keep = jnp.exp2(old - new)
         max_s[...] = new
         p = jnp.exp2(s * factor - new)
-        sum_s[...] = sum_s[...] * keep + jnp.sum(p, axis=0, keepdims=True)
-        mixed = dot(kv_ref[t, :, :, 16:32, :].reshape(TILE, LANES), p.astype(jnp.bfloat16), 0, 0)
-        acc_s[...] = acc_s[...] * keep + mixed
+        values = kv_ref[t, :, :, 16:32, :].reshape(TILE, LANES)
+        ones = jnp.ones((8, TILE), jnp.bfloat16)
+        values = jnp.concatenate([values.T, ones], axis=0)
+        acc_s[...] = acc_s[...] * keep + dot(values, p.astype(jnp.bfloat16), 1, 0)
 
     def absorb_last(t, s_ref):
         s = s_ref[...] + jnp.concatenate([mask_s[...]] * GROUP, axis=1)
@@ -129,21 +129,21 @@
             last = zh * 4 + xb
             meta = q_ref[pl.ds(xb * 8, 8), GROUP * 16 :, :].astype(jnp.float32)
             pos = jnp.sum(meta, axis=0)[0:1]
-            pick = (down.astype(jnp.float32) == pos).astype(jnp.float32).astype(jnp.bfloat16)
             for g in range(GROUP):
-                raw = q_ref[pl.ds(xb * 8, 8), g * 16 : (g + 1) * 16, :].reshape(BLOCK, LANES)
-                q_s[:, g * BLOCK : (g + 1) * BLOCK] = dot(raw, pick, 0, 1).astype(jnp.bfloat16)
-            reach = (down <= across) & (block * BLOCK + down < live)
-            seen = dot(pick, reach.astype(jnp.float32).astype(jnp.bfloat16), 0, 0)
-            mask_s[0:BLOCK, :] = jnp.where(seen > 0.5, 0.0, NEG)
+                raw = q_ref[pl.ds(xb * 8, 8), g * 16 : (g + 1) * 16, :]
+                q_s[:, g * BLOCK : (g + 1) * BLOCK] = raw.reshape(BLOCK, LANES).T
+            query_pos = jnp.broadcast_to(pos, (BLOCK, LANES))
+            key_pos = query_pos.T
+            live_rows = (live - block * BLOCK).astype(jnp.float32)
+            reach = (key_pos <= query_pos) & (key_pos < live_rows)
+            mask_s[0:BLOCK, :] = jnp.where(reach, 0.0, NEG)
             for a, by in ((1, 3), (2, 1), (3, 2)):
                 before = jnp.bitwise_and(y + by, 3) < y
                 mask_s[a * BLOCK : (a + 1) * BLOCK, :] = jnp.full(
                     (BLOCK, LANES), jnp.where(before, 0.0, NEG)
                 )
             max_s[...] = jnp.full((1, rows), NEG, jnp.float32)
-            sum_s[...] = jnp.zeros((1, rows), jnp.float32)
-            acc_s[...] = jnp.zeros((LANES, rows), jnp.float32)
+            acc_s[...] = jnp.zeros((LANES + 8, rows), jnp.float32)
 
             scores(first, s0, top0)
             full = last - first
@@ -169,14 +169,28 @@
             def _():
                 absorb_last(last, s0)
 
-            out = acc_s[...] / sum_s[...]
-            row_live = block * BLOCK + down < live
+            pick = (down.astype(jnp.float32) == pos).astype(jnp.float32).astype(jnp.bfloat16)
+            scale = 1.0 / acc_s[LANES : LANES + 1, :]
             for g in range(GROUP):
-                piece = jnp.where(row_live, out[:, g * BLOCK : (g + 1) * BLOCK].T, 0.0)
-                out_ref[0, :, g * LANES : (g + 1) * LANES] = piece.astype(jnp.bfloat16)
+                at = slice(g * BLOCK, (g + 1) * BLOCK)
+                piece = jnp.where(pos < live_rows, acc_s[0:LANES, at] * scale[:, at], 0.0)
+                out_ref[0, :, g * LANES : (g + 1) * LANES] = dot(
+                    pick, piece.astype(jnp.bfloat16), 1, 1
+                ).astype(jnp.bfloat16)
 
     for out_ref, k in zip(out_refs, shifts):
         one_block(out_ref, jnp.bitwise_xor(x, k))
+
+
+def attend_scratch():
+    rows = GROUP * BLOCK
+    wide = pltpu.VMEM((TILE, rows), jnp.float32)
+    top = pltpu.VMEM((8, rows), jnp.float32)
+    line = pltpu.VMEM((1, rows), jnp.float32)
+    queries = pltpu.VMEM((LANES, rows), jnp.bfloat16)
+    mask = pltpu.VMEM((TILE, LANES), jnp.float32)
+    total = pltpu.VMEM((LANES + 8, rows), jnp.float32)
+    return [queries, mask, wide, wide, top, top, line, total]
 
 
 def join_kernel(a_ref, b_ref, c_ref, d_ref, out_ref):
@@ -260,25 +274,12 @@
 
     def attend(shifts):
         rows = GROUP * BLOCK
-        wide = pltpu.VMEM((TILE, rows), jnp.float32)
-        top = pltpu.VMEM((8, rows), jnp.float32)
-        line = pltpu.VMEM((1, rows), jnp.float32)
         return pl.pallas_call(
             functools.partial(attend_kernel, shifts),
             out_shape=[jax.ShapeDtypeStruct((1, BLOCK, rows), jnp.bfloat16)] * len(shifts),
             in_specs=[smem(), vmem(), vmem()],
             out_specs=[vmem()] * len(shifts),
-            scratch_shapes=[
-                pltpu.VMEM((LANES, rows), jnp.bfloat16),
-                pltpu.VMEM((TILE, LANES), jnp.float32),
-                wide,
-                wide,
-                top,
-                top,
-                line,
-                line,
-                pltpu.VMEM((LANES, rows), jnp.float32),
-            ],
+            scratch_shapes=attend_scratch(),
             compiler_params=params(),
             cost_estimate=pl.CostEstimate(
                 flops=2 * 2 * rows * 4096 * LANES,
@@ -289,7 +290,7 @@
         )(video_frames, q_got, tiles)
 
     parts = {}
-    for pair in ((1, 2), (3,), (0,)):
+    for pair in ((2,), (1, 3), (0,)):
         blocks = attend(pair)
         for part, k in zip(blocks, pair):
             parts[k] = swap(part, k) if k else part

time: 91.4 us -> 89.2 us (0.976)
  the two profiles are of different devices: /device:TPU:198 before, /device:TPU:224 now
where the time goes in v4:
time: 89.2 us; the launch traced here: 88.3 us
  waiting for transfers between devices  35.9 us (40%)
  starting transfers between devices  30.6 us (34%)
  Pallas kernels  21.7 us (24%)
    ppermute x4, waiting for transfers between devices, shift(): return lax.ppermute(value, axis, [(i, (i + by) % 4) for i in range(4)])  19.9 us
    all_to_all x2, starting transfers between devices, exchange(): return lax.all_to_all(value, axes, split_axis=0, concat_axis=0, tiled=True)  16 us
    pallas_call x3, Pallas kernels, attend(): pl.pallas_call(functools.partial(attend_kernel, shifts), out_shape=[jax.S...  15.9 us
    all_to_all x2, waiting for transfers between devices, exchange(): return lax.all_to_all(value, axes, split_axis=0, concat_axis=0, tiled=True)  13.3 us
    ppermute x3, starting transfers between devices, swap(): return lax.ppermute(value, 'x', [(i, i ^ k) for i in range(4)])  7.61 us
    ppermute x4, starting transfers between devices, shift(): return lax.ppermute(value, axis, [(i, (i + by) % 4) for i in range(4)])  6.94 us
    ppermute x3, waiting for transfers between devices, swap(): return lax.ppermute(value, 'x', [(i, i ^ k) for i in range(4)])  2.61 us
    pallas_call x1, Pallas kernels, local(): pl.pallas_call(prep_q_kernel, out_shape=jax.ShapeDtypeStruct((32, GROUP *...  2.58 us
  transfers between devices with their start and end apart: 9, of which 5 were waited for; matrix products, arithmetic and copies ran while one was open for 0% of the time, Pallas kernels for 15%

profile of v4, /device:TPU:224, one launch (start us, length us, event | category | flops | bytes accessed | tf_op | source)
XLA Modules:
  0.0 88.3 jit_solution(15866327619492337726)
XLA Ops:
  0.0 2.1 %prep_kv.1 = bf16[64,32,128]{2,1,0:T(8,128)(2,1)} custom-call(s32[1,16]{1,0:T(1,128)} %sec_ref.3, bf16[1,16,8,512]{3,2,1,0:T(8,128)(2,1)} %k_ref.1, bf16[1,16,8,512]{3,2,1,0:T(8,128)(2,1)} %v_ref.1), custom_call_target="tpu_custom_call" | custom-call | tf_op jit(solution)/shard_map/prep_kv/pallas_call | solution.py:242
  2.1 9.0 %all-to-all-start = ((bf16[64,32,128]{2,1,0:T(8,128)(2,1)}), bf16[64,32,128]{2,1,0:T(8,128)(2,1)S(1)}, u32[]{:S(2)}, u32[]{:S(2)}) async-start(bf16[64,32,128]{2,1,0:T(8,128)(2,1)} %prep_kv.1), calls=%async_computation | async-start | bytes 1048576 | tf_op jit(solution)/shard_map/all_to_all | solution.py:221
  11.1 2.6 %prep_q.1 = bf16[32,120,128]{2,1,0:T(8,128)(2,1)} custom-call(s32[1,16]{1,0:T(1,128)} %sec_ref.3, s32[1,16]{1,0:T(1,128)} %off_ref.1, bf16[1,16,8,3584]{3,2,1,0:T(8,128)(2,1)} %q_ref.1), custom_call_target="tpu_custom_call" | custom-call | tf_op jit(solution)/shard_map/prep_q/pallas_call | solution.py:251
  13.6 13.3 %all-to-all-done.refs_0_ = bf16[64,32,128]{2,1,0:T(8,128)(2,1)S(1)} async-done(((bf16[64,32,128]{2,1,0:T(8,128)(2,1)}), bf16[64,32,128]{2,1,0:T(8,128)(2,1)S(1)}, u32[]{:S(2)}, u32[]{:S(2)}) %all-to-all-start) | async-done | bytes 524320 | tf_op jit(solution)/shard_map/all_to_all | solution.py:221
  27.0 7.0 %all-to-all-start.1 = ((bf16[32,120,128]{2,1,0:T(8,128)(2,1)}), bf16[32,120,128]{2,1,0:T(8,128)(2,1)}, u32[]{:S(2)}, u32[]{:S(2)}) async-start(bf16[32,120,128]{2,1,0:T(8,128)(2,1)} %prep_q.1), calls=%async_computation.1 | async-start | bytes 1966080 | tf_op jit(solution)/shard_map/all_to_all | solution.py:221
  34.0 3.1 %collective-permute-start.1 = (bf16[64,32,128]{2,1,0:T(8,128)(2,1)S(1)}, bf16[64,32,128]{2,1,0:T(8,128)(2,1)S(1)}, u32[]{:S(2)}, u32[]{:S(2)}) collective-permute-start(bf16[64,32,128]{2,1,0:T(8,128)(2,1)S(1)} %all-to-all-done.refs_0_), channel_id=1, source_target_pairs={{0,3},{1,0},{2,1},{3,2},{4,7},{5,4},{6,5},{7,6},{8,11},{9,8},{10,9... | collective-permute-start | bytes 1572872 | tf_op jit(solution)/shard_map/ppermute | solution.py:225
  37.1 0.0 collective-permute-start
  37.1 11.5 %collective-permute-done.1.refs_2_ = bf16[64,32,128]{2,1,0:T(8,128)(2,1)S(1)} collective-permute-done((bf16[64,32,128]{2,1,0:T(8,128)(2,1)S(1)}, bf16[64,32,128]{2,1,0:T(8,128)(2,1)S(1)}, u32[]{:S(2)}, u32[]{:S(2)}) %collective-permute-start.1) | collective-permute-done | bytes 524320 | tf_op jit(solution)/shard_map/ppermute | solution.py:225
  48.6 3.8 %collective-permute-start.3 = (bf16[64,16,128]{2,1,0:T(8,128)(2,1)S(1)}, bf16[64,16,128]{2,1,0:T(8,128)(2,1)S(1)}, u32[]{:S(2)}, u32[]{:S(2)}) collective-permute-start(bf16[64,16,128]{2,1,0:T(8,128)(2,1)S(1)} %slice.9), channel_id=1, source_target_pairs={{0,3},{1,0},{2,1},{3,2},{4,7},{5,4},{6,5},{7,6},{8,11},{9,8},{10,9... | collective-permute-start | bytes 786440 | tf_op jit(solution)/shard_map/ppermute | solution.py:225
  52.4 0.0 collective-permute-done.refs_1_
  52.4 0.0 copy-start
  52.4 0.1 collective-permute-start.2
  52.5 4.9 %collective-permute-done.3.refs_4_ = bf16[64,16,128]{2,1,0:T(8,128)(2,1)S(1)} collective-permute-done((bf16[64,16,128]{2,1,0:T(8,128)(2,1)S(1)}, bf16[64,16,128]{2,1,0:T(8,128)(2,1)S(1)}, u32[]{:S(2)}, u32[]{:S(2)}) %collective-permute-start.3) | collective-permute-done | bytes 262176 | tf_op jit(solution)/shard_map/ppermute | solution.py:225
  57.4 3.5 %collective-permute-done.2.refs_3_ = bf16[64,16,128]{2,1,0:T(8,128)(2,1)S(1)} collective-permute-done((bf16[64,16,128]{2,1,0:T(8,128)(2,1)S(1)}, bf16[64,16,128]{2,1,0:T(8,128)(2,1)S(1)}, u32[]{:S(2)}, u32[]{:S(2)}) %collective-permute-start.2) | collective-permute-done | bytes 262176 | tf_op jit(solution)/shard_map/ppermute | solution.py:225
  61.0 0.1 arrange.1.kv_ref
  61.1 0.0 all-to-all-done.1.q_ref
  61.1 0.0 copy-done
  61.1 5.3 %attend.4 = (bf16[1,128,896]{2,1,0:T(8,128)(2,1)S(1)}, bf16[1,128,896]{2,1,0:T(8,128)(2,1)S(1)}) custom-call(s32[8]{0:T(128)S(1)} %copy-done, bf16[32,120,128]{2,1,0:T(8,128)(2,1)} %all-to-all-done.1.q_ref, bf16[8,4,8,32,128]{4,3,2,1,0:T(8,128)(2,1)S(1)} %arrange.1.kv_ref), custom_call_target="tpu_custom_call" | custom-call | flops 1879048192 | bytes 3145728 | tf_op jit(solution)/shard_map/attend/pallas_call | solution.py:277
  66.4 5.9 %collective-permute-start.4 = (bf16[1,128,896]{2,1,0:T(8,128)(2,1)S(1)}, bf16[1,128,896]{2,1,0:T(8,128)(2,1)S(1)}, u32[]{:S(2)}, u32[]{:S(2)}) collective-permute-start(bf16[1,128,896]{2,1,0:T(8,128)(2,1)S(1)} %get-tuple-element.11), channel_id=1, source_target_pairs={{0,4},{4,0},{8,12},{12,8},{1,5},{5,1},{9,13},{13,9},{2,6},{6,2},{1... | collective-permute-start | bytes 688136 | tf_op jit(solution)/shard_map/ppermute | solution.py:229
  72.2 1.6 %collective-permute-start.6 = (bf16[1,128,896]{2,1,0:T(8,128)(2,1)S(1)}, bf16[1,128,896]{2,1,0:T(8,128)(2,1)S(1)}, u32[]{:S(2)}, u32[]{:S(2)}) collective-permute-start(bf16[1,128,896]{2,1,0:T(8,128)(2,1)S(1)} %get-tuple-element.12), channel_id=1, source_target_pairs={{0,12},{4,8},{8,4},{12,0},{1,13},{5,9},{9,5},{13,1},{2,14},{6,10},... | collective-permute-start | bytes 688136 | tf_op jit(solution)/shard_map/ppermute | solution.py:229
  73.8 5.9 %attend.5 = bf16[1,128,896]{2,1,0:T(8,128)(2,1)S(1)} custom-call(s32[8]{0:T(128)S(1)} %copy-done, bf16[32,120,128]{2,1,0:T(8,128)(2,1)} %all-to-all-done.1.q_ref, bf16[8,4,8,32,128]{4,3,2,1,0:T(8,128)(2,1)S(1)} %arrange.1.kv_ref), custom_call_target="tpu_custom_call" | custom-call | flops 1879048192 | bytes 3145728 | tf_op jit(solution)/shard_map/attend/pallas_call | solution.py:277
  79.7 0.2 collective-permute-start.5
  79.9 4.8 %attend.3.a_ref = bf16[1,128,896]{2,1,0:T(8,128)(2,1)S(1)} custom-call(s32[8]{0:T(128)S(1)} %copy-done, bf16[32,120,128]{2,1,0:T(8,128)(2,1)} %all-to-all-done.1.q_ref, bf16[8,4,8,32,128]{4,3,2,1,0:T(8,128)(2,1)S(1)} %arrange.1.kv_ref), custom_call_target="tpu_custom_call" | custom-call | flops 1879048192 | bytes 3145728 | tf_op jit(solution)/shard_map/attend/pallas_call | solution.py:277
  84.7 0.0 collective-permute-done.4.b_ref
  84.7 0.0 collective-permute-done.6.d_ref
  84.7 2.6 %collective-permute-done.5.c_ref = bf16[1,128,896]{2,1,0:T(8,128)(2,1)S(1)} collective-permute-done((bf16[1,128,896]{2,1,0:T(8,128)(2,1)S(1)}, bf16[1,128,896]{2,1,0:T(8,128)(2,1)S(1)}, u32[]{:S(2)}, u32[]{:S(2)}) %collective-permute-start.5) | collective-permute-done | bytes 229408 | tf_op jit(solution)/shard_map/ppermute | solution.py:229
  87.3 1.0 %join.1 = bf16[1,128,3584]{2,1,0:T(8,128)(2,1)} custom-call(bf16[1,128,896]{2,1,0:T(8,128)(2,1)S(1)} %attend.3.a_ref, bf16[1,128,896]{2,1,0:T(8,128)(2,1)S(1)} %collective-permute-done.4.b_ref, bf16[1,128,896]{2,1,0:T(8,128)(2,1)S(1)} %collective-permute-done.5.c_ref, bf16[1,128,896]{2,1,0:T(8,128)(2,1)S(1)} %collective-permute-done.6.d_ref), custom_call_target="tpu_custom_call" | custom-call | tf_op jit(solution)/shard_map/join/pallas_call | solution.py:297
  (2 shorter events, 0.0 us)
Async XLA Ops:
  2.1 24.9 %all-to-all-start = ((bf16[64,32,128]{2,1,0:T(8,128)(2,1)}), bf16[64,32,128]{2,1,0:T(8,128)(2,1)S(1)}, u32[]{:S(2)}, u32[]{:S(2)}) async-start(bf16[64,32,128]{2,1,0:T(8,128)(2,1)} %prep_kv.1), calls=%async_computation | async-start | bytes 1048576 | tf_op jit(solution)/shard_map/all_to_all | solution.py:221
  27.0 34.1 %all-to-all-start.1 = ((bf16[32,120,128]{2,1,0:T(8,128)(2,1)}), bf16[32,120,128]{2,1,0:T(8,128)(2,1)}, u32[]{:S(2)}, u32[]{:S(2)}) async-start(bf16[32,120,128]{2,1,0:T(8,128)(2,1)} %prep_q.1), calls=%async_computation.1 | async-start | bytes 1966080 | tf_op jit(solution)/shard_map/all_to_all | solution.py:221
  34.0 14.6 %collective-permute-start.1 = (bf16[64,32,128]{2,1,0:T(8,128)(2,1)S(1)}, bf16[64,32,128]{2,1,0:T(8,128)(2,1)S(1)}, u32[]{:S(2)}, u32[]{:S(2)}) collective-permute-start(bf16[64,32,128]{2,1,0:T(8,128)(2,1)S(1)} %all-to-all-done.refs_0_), channel_id=1, source_target_pairs={{0,3},{1,0},{2,1},{3,2},{4,7},{5,4},{6,5},{7,6},{8,11},{9,8},{10,9... | collective-permute-start | bytes 1572872 | tf_op jit(solution)/shard_map/ppermute | solution.py:225
  37.1 15.3 %collective-permute-start = (bf16[64,32,128]{2,1,0:T(8,128)(2,1)S(1)}, bf16[64,32,128]{2,1,0:T(8,128)(2,1)S(1)}, u32[]{:S(2)}, u32[]{:S(2)}) collective-permute-start(bf16[64,32,128]{2,1,0:T(8,128)(2,1)S(1)} %all-to-all-done.refs_0_), channel_id=1, source_target_pairs={{0,1},{1,2},{2,3},{3,0},{4,5},{5,6},{6,7},{7,4},{8,9},{9,10},{10,1... | collective-permute-start | bytes 1572872 | tf_op jit(solution)/shard_map/ppermute | solution.py:225
  48.6 8.8 %collective-permute-start.3 = (bf16[64,16,128]{2,1,0:T(8,128)(2,1)S(1)}, bf16[64,16,128]{2,1,0:T(8,128)(2,1)S(1)}, u32[]{:S(2)}, u32[]{:S(2)}) collective-permute-start(bf16[64,16,128]{2,1,0:T(8,128)(2,1)S(1)} %slice.9), channel_id=1, source_target_pairs={{0,3},{1,0},{2,1},{3,2},{4,7},{5,4},{6,5},{7,6},{8,11},{9,8},{10,9... | collective-permute-start | bytes 786440 | tf_op jit(solution)/shard_map/ppermute | solution.py:225
  52.4 8.7 %copy-start = (s32[8]{0:T(128)S(1)}, s32[8]{0:T(128)}, u32[]{:S(2)}) copy-start(s32[8]{0:T(128)} %video_ref.5) | copy-start | bytes 100
  52.4 8.5 %collective-permute-start.2 = (bf16[64,16,128]{2,1,0:T(8,128)(2,1)S(1)}, bf16[64,16,128]{2,1,0:T(8,128)(2,1)S(1)}, u32[]{:S(2)}, u32[]{:S(2)}) collective-permute-start(bf16[64,16,128]{2,1,0:T(8,128)(2,1)S(1)} %slice.8), channel_id=1, source_target_pairs={{0,1},{1,2},{2,3},{3,0},{4,5},{5,6},{6,7},{7,4},{8,9},{9,10},{10,1... | collective-permute-start | bytes 786440 | tf_op jit(solution)/shard_map/ppermute | solution.py:225
  66.4 18.3 %collective-permute-start.4 = (bf16[1,128,896]{2,1,0:T(8,128)(2,1)S(1)}, bf16[1,128,896]{2,1,0:T(8,128)(2,1)S(1)}, u32[]{:S(2)}, u32[]{:S(2)}) collective-permute-start(bf16[1,128,896]{2,1,0:T(8,128)(2,1)S(1)} %get-tuple-element.11), channel_id=1, source_target_pairs={{0,4},{4,0},{8,12},{12,8},{1,5},{5,1},{9,13},{13,9},{2,6},{6,2},{1... | collective-permute-start | bytes 688136 | tf_op jit(solution)/shard_map/ppermute | solution.py:229
  72.2 12.5 %collective-permute-start.6 = (bf16[1,128,896]{2,1,0:T(8,128)(2,1)S(1)}, bf16[1,128,896]{2,1,0:T(8,128)(2,1)S(1)}, u32[]{:S(2)}, u32[]{:S(2)}) collective-permute-start(bf16[1,128,896]{2,1,0:T(8,128)(2,1)S(1)} %get-tuple-element.12), channel_id=1, source_target_pairs={{0,12},{4,8},{8,4},{12,0},{1,13},{5,9},{9,5},{13,1},{2,14},{6,10},... | collective-permute-start | bytes 688136 | tf_op jit(solution)/shard_map/ppermute | solution.py:229
  79.7 7.6 %collective-permute-start.5 = (bf16[1,128,896]{2,1,0:T(8,128)(2,1)S(1)}, bf16[1,128,896]{2,1,0:T(8,128)(2,1)S(1)}, u32[]{:S(2)}, u32[]{:S(2)}) collective-permute-start(bf16[1,128,896]{2,1,0:T(8,128)(2,1)S(1)} %attend.5), channel_id=1, source_target_pairs={{0,8},{4,12},{8,0},{12,4},{1,9},{5,13},{9,1},{13,5},{2,10},{6,14},... | collective-permute-start | bytes 688136 | tf_op jit(solution)/shard_map/ppermute | solution.py:229

commit v5 on v4

--- a/solution.py
+++ b/solution.py
@@ -82,10 +82,15 @@
     shifts, video_ref, q_ref, kv_ref, *refs
 ):
     out_refs = refs[: len(shifts)]
-    q_s, mask_s, s0, s1, top0, top1, max_s, acc_s = refs[len(shifts) :]
+    got_s, q_s, mask_s, s0, s1, top0, top1, max_s, acc_s, sem = refs[len(shifts) :]
     x, y, zh = lax.axis_index("x"), lax.axis_index("y"), lax.axis_index("zh")
     me = lax.axis_index("zl") * 2 + lax.axis_index("core")
     live = video_ref[me] * 8
+    copies = []
+    for i, k in enumerate(shifts):
+        at = pl.ds(jnp.bitwise_xor(x, k) * 8, 8)
+        copies.append(pltpu.make_async_copy(q_ref.at[at], got_s.at[i], sem.at[i]))
+        copies[-1].start()
     rows = GROUP * BLOCK
     factor = math.log2(math.e) / math.sqrt(128.0)
     down = lax.broadcasted_iota(jnp.int32, (BLOCK, LANES), 0)
@@ -115,7 +120,7 @@
         s = s_ref[...] + jnp.concatenate([mask_s[...]] * GROUP, axis=1)
         absorb(t, s, jnp.max(s.reshape(TILE // 8, 8, rows), axis=0))
 
-    def one_block(out_ref, xb):
+    def one_block(out_ref, got_ref, xb):
         block = zh * 16 + xb * 4 + y
         block_live = block * BLOCK < live
 
@@ -127,10 +132,10 @@
         def _():
             first = 0
             last = zh * 4 + xb
-            meta = q_ref[pl.ds(xb * 8, 8), GROUP * 16 :, :].astype(jnp.float32)
+            meta = got_ref[:, GROUP * 16 :, :].astype(jnp.float32)
             pos = jnp.sum(meta, axis=0)[0:1]
             for g in range(GROUP):
-                raw = q_ref[pl.ds(xb * 8, 8), g * 16 : (g + 1) * 16, :]
+                raw = got_ref[:, g * 16 : (g + 1) * 16, :]
                 q_s[:, g * BLOCK : (g + 1) * BLOCK] = raw.reshape(BLOCK, LANES).T
             query_pos = jnp.broadcast_to(pos, (BLOCK, LANES))
             key_pos = query_pos.T
@@ -178,11 +183,12 @@
                     pick, piece.astype(jnp.bfloat16), 1, 1
                 ).astype(jnp.bfloat16)
 
-    for out_ref, k in zip(out_refs, shifts):
-        one_block(out_ref, jnp.bitwise_xor(x, k))
-
-
-def attend_scratch():
+    for i, k in enumerate(shifts):
+        copies[i].wait()
+        one_block(out_refs[i], got_s.at[i], jnp.bitwise_xor(x, k))
+
+
+def attend_scratch(blocks):
     rows = GROUP * BLOCK
     wide = pltpu.VMEM((TILE, rows), jnp.float32)
     top = pltpu.VMEM((8, rows), jnp.float32)
@@ -190,7 +196,9 @@
     queries = pltpu.VMEM((LANES, rows), jnp.bfloat16)
     mask = pltpu.VMEM((TILE, LANES), jnp.float32)
     total = pltpu.VMEM((LANES + 8, rows), jnp.float32)
-    return [queries, mask, wide, wide, top, top, line, total]
+    got = pltpu.VMEM((blocks, 8, GROUP * 16 + 8, LANES), jnp.bfloat16)
+    sem = pltpu.SemaphoreType.DMA((blocks,))
+    return [got, queries, mask, wide, wide, top, top, line, total, sem]
 
 
 def join_kernel(a_ref, b_ref, c_ref, d_ref, out_ref):
@@ -277,9 +285,9 @@
         return pl.pallas_call(
             functools.partial(attend_kernel, shifts),
             out_shape=[jax.ShapeDtypeStruct((1, BLOCK, rows), jnp.bfloat16)] * len(shifts),
-            in_specs=[smem(), vmem(), vmem()],
+            in_specs=[smem(), anywhere(), vmem()],
             out_specs=[vmem()] * len(shifts),
-            scratch_shapes=attend_scratch(),
+            scratch_shapes=attend_scratch(len(shifts)),
             compiler_params=params(),
             cost_estimate=pl.CostEstimate(
                 flops=2 * 2 * rows * 4096 * LANES,

time: 89.2 us -> 89.4 us (level)
  the two profiles are of different devices: /device:TPU:224 before, /device:TPU:128 now
where the time goes in v5:
time: 89.4 us; the launch traced here: 88.9 us
  waiting for transfers between devices  34.9 us (39%)
  Pallas kernels  27.6 us (31%)
  starting transfers between devices  26.3 us (29%)
    pallas_call x3, Pallas kernels, attend(): pl.pallas_call(functools.partial(attend_kernel, shifts), out_shape=[jax.S...  21.8 us
    ppermute x4, waiting for transfers between devices, shift(): return lax.ppermute(value, axis, [(i, (i + by) % 4) for i in range(4)])  20.2 us
    all_to_all x2, starting transfers between devices, exchange(): return lax.all_to_all(value, axes, split_axis=0, concat_axis=0, tiled=True)  15.5 us
    all_to_all x2, waiting for transfers between devices, exchange(): return lax.all_to_all(value, axes, split_axis=0, concat_axis=0, tiled=True)  12.3 us
    ppermute x4, starting transfers between devices, shift(): return lax.ppermute(value, axis, [(i, (i + by) % 4) for i in range(4)])  6.95 us
    ppermute x3, starting transfers between devices, swap(): return lax.ppermute(value, 'x', [(i, i ^ k) for i in range(4)])  3.86 us
    pallas_call x1, Pallas kernels, local(): pl.pallas_call(prep_q_kernel, out_shape=jax.ShapeDtypeStruct((32, GROUP *...  2.58 us
    ppermute x3, waiting for transfers between devices, swap(): return lax.ppermute(value, 'x', [(i, i ^ k) for i in range(4)])  2.42 us
  transfers between devices with their start and end apart: 9, of which 5 were waited for; matrix products, arithmetic and copies ran while one was open for 0% of the time, Pallas kernels for 16%

profile of v5, /device:TPU:128, one launch (start us, length us, event | category | flops | bytes accessed | tf_op | source)
XLA Modules:
  0.0 88.9 jit_solution(8185921278382911151)
XLA Ops:
  0.0 2.1 %prep_kv.1 = bf16[64,32,128]{2,1,0:T(8,128)(2,1)} custom-call(s32[1,16]{1,0:T(1,128)} %sec_ref.3, bf16[1,16,8,512]{3,2,1,0:T(8,128)(2,1)} %k_ref.1, bf16[1,16,8,512]{3,2,1,0:T(8,128)(2,1)} %v_ref.1), custom_call_target="tpu_custom_call" | custom-call | tf_op jit(solution)/shard_map/prep_kv/pallas_call | solution.py:250
  2.1 10.3 %all-to-all-start = ((bf16[64,32,128]{2,1,0:T(8,128)(2,1)}), bf16[64,32,128]{2,1,0:T(8,128)(2,1)S(1)}, u32[]{:S(2)}, u32[]{:S(2)}) async-start(bf16[64,32,128]{2,1,0:T(8,128)(2,1)} %prep_kv.1), calls=%async_computation | async-start | bytes 1048576 | tf_op jit(solution)/shard_map/all_to_all | solution.py:229
  12.4 2.6 %prep_q.1 = bf16[32,120,128]{2,1,0:T(8,128)(2,1)} custom-call(s32[1,16]{1,0:T(1,128)} %sec_ref.3, s32[1,16]{1,0:T(1,128)} %off_ref.1, bf16[1,16,8,3584]{3,2,1,0:T(8,128)(2,1)} %q_ref.1), custom_call_target="tpu_custom_call" | custom-call | tf_op jit(solution)/shard_map/prep_q/pallas_call | solution.py:259
  15.0 12.3 %all-to-all-done.refs_0_ = bf16[64,32,128]{2,1,0:T(8,128)(2,1)S(1)} async-done(((bf16[64,32,128]{2,1,0:T(8,128)(2,1)}), bf16[64,32,128]{2,1,0:T(8,128)(2,1)S(1)}, u32[]{:S(2)}, u32[]{:S(2)}) %all-to-all-start) | async-done | bytes 524320 | tf_op jit(solution)/shard_map/all_to_all | solution.py:229
  27.3 5.1 %all-to-all-start.1 = ((bf16[32,120,128]{2,1,0:T(8,128)(2,1)}), bf16[32,120,128]{2,1,0:T(8,128)(2,1)}, u32[]{:S(2)}, u32[]{:S(2)}) async-start(bf16[32,120,128]{2,1,0:T(8,128)(2,1)} %prep_q.1), calls=%async_computation.1 | async-start | bytes 1966080 | tf_op jit(solution)/shard_map/all_to_all | solution.py:229
  32.4 3.1 %collective-permute-start.1 = (bf16[64,32,128]{2,1,0:T(8,128)(2,1)S(1)}, bf16[64,32,128]{2,1,0:T(8,128)(2,1)S(1)}, u32[]{:S(2)}, u32[]{:S(2)}) collective-permute-start(bf16[64,32,128]{2,1,0:T(8,128)(2,1)S(1)} %all-to-all-done.refs_0_), channel_id=1, source_target_pairs={{0,3},{1,0},{2,1},{3,2},{4,7},{5,4},{6,5},{7,6},{8,11},{9,8},{10,9... | collective-permute-start | bytes 1572872 | tf_op jit(solution)/shard_map/ppermute | solution.py:233
  35.5 0.0 collective-permute-start
  35.5 11.6 %collective-permute-done.1.refs_2_ = bf16[64,32,128]{2,1,0:T(8,128)(2,1)S(1)} collective-permute-done((bf16[64,32,128]{2,1,0:T(8,128)(2,1)S(1)}, bf16[64,32,128]{2,1,0:T(8,128)(2,1)S(1)}, u32[]{:S(2)}, u32[]{:S(2)}) %collective-permute-start.1) | collective-permute-done | bytes 524320 | tf_op jit(solution)/shard_map/ppermute | solution.py:233
  47.1 3.8 %collective-permute-start.3 = (bf16[64,16,128]{2,1,0:T(8,128)(2,1)S(1)}, bf16[64,16,128]{2,1,0:T(8,128)(2,1)S(1)}, u32[]{:S(2)}, u32[]{:S(2)}) collective-permute-start(bf16[64,16,128]{2,1,0:T(8,128)(2,1)S(1)} %slice.9), channel_id=1, source_target_pairs={{0,3},{1,0},{2,1},{3,2},{4,7},{5,4},{6,5},{7,6},{8,11},{9,8},{10,9... | collective-permute-start | bytes 786440 | tf_op jit(solution)/shard_map/ppermute | solution.py:233
  50.8 0.0 collective-permute-done.refs_1_
  50.9 0.0 copy-start
  50.9 0.1 collective-permute-start.2
  51.0 5.1 %collective-permute-done.3.refs_4_ = bf16[64,16,128]{2,1,0:T(8,128)(2,1)S(1)} collective-permute-done((bf16[64,16,128]{2,1,0:T(8,128)(2,1)S(1)}, bf16[64,16,128]{2,1,0:T(8,128)(2,1)S(1)}, u32[]{:S(2)}, u32[]{:S(2)}) %collective-permute-start.3) | collective-permute-done | bytes 262176 | tf_op jit(solution)/shard_map/ppermute | solution.py:233
  56.1 3.5 %collective-permute-done.2.refs_3_ = bf16[64,16,128]{2,1,0:T(8,128)(2,1)S(1)} collective-permute-done((bf16[64,16,128]{2,1,0:T(8,128)(2,1)S(1)}, bf16[64,16,128]{2,1,0:T(8,128)(2,1)S(1)}, u32[]{:S(2)}, u32[]{:S(2)}) %collective-permute-start.2) | collective-permute-done | bytes 262176 | tf_op jit(solution)/shard_map/ppermute | solution.py:233
  59.6 0.1 arrange.1.kv_ref
  59.7 0.0 all-to-all-done.1.q_ref
  59.8 0.0 copy-done
  59.8 10.6 %attend.4 = (bf16[1,128,896]{2,1,0:T(8,128)(2,1)S(1)}, bf16[1,128,896]{2,1,0:T(8,128)(2,1)S(1)}) custom-call(s32[8]{0:T(128)S(1)} %copy-done, bf16[32,120,128]{2,1,0:T(8,128)(2,1)} %all-to-all-done.1.q_ref, bf16[8,4,8,32,128]{4,3,2,1,0:T(8,128)(2,1)S(1)} %arrange.1.kv_ref), custom_call_target="tpu_custom_call" | custom-call | flops 1879048192 | bytes 3145728 | tf_op jit(solution)/shard_map/attend/pallas_call | solution.py:285
  70.3 0.8 collective-permute-start.4
  71.1 3.0 %collective-permute-start.6 = (bf16[1,128,896]{2,1,0:T(8,128)(2,1)S(1)}, bf16[1,128,896]{2,1,0:T(8,128)(2,1)S(1)}, u32[]{:S(2)}, u32[]{:S(2)}) collective-permute-start(bf16[1,128,896]{2,1,0:T(8,128)(2,1)S(1)} %get-tuple-element.12), channel_id=1, source_target_pairs={{0,12},{4,8},{8,4},{12,0},{1,13},{5,9},{9,5},{13,1},{2,14},{6,10},... | collective-permute-start | bytes 688136 | tf_op jit(solution)/shard_map/ppermute | solution.py:237
  74.1 6.2 %attend.5 = bf16[1,128,896]{2,1,0:T(8,128)(2,1)S(1)} custom-call(s32[8]{0:T(128)S(1)} %copy-done, bf16[32,120,128]{2,1,0:T(8,128)(2,1)} %all-to-all-done.1.q_ref, bf16[8,4,8,32,128]{4,3,2,1,0:T(8,128)(2,1)S(1)} %arrange.1.kv_ref), custom_call_target="tpu_custom_call" | custom-call | flops 1879048192 | bytes 3145728 | tf_op jit(solution)/shard_map/attend/pallas_call | solution.py:285
  80.3 0.1 collective-permute-start.5
  80.4 5.1 %attend.3.a_ref = bf16[1,128,896]{2,1,0:T(8,128)(2,1)S(1)} custom-call(s32[8]{0:T(128)S(1)} %copy-done, bf16[32,120,128]{2,1,0:T(8,128)(2,1)} %all-to-all-done.1.q_ref, bf16[8,4,8,32,128]{4,3,2,1,0:T(8,128)(2,1)S(1)} %arrange.1.kv_ref), custom_call_target="tpu_custom_call" | custom-call | flops 1879048192 | bytes 3145728 | tf_op jit(solution)/shard_map/attend/pallas_call | solution.py:285
  85.4 0.0 collective-permute-done.4.b_ref
  85.4 0.0 collective-permute-done.6.d_ref
  85.5 2.4 %collective-permute-done.5.c_ref = bf16[1,128,896]{2,1,0:T(8,128)(2,1)S(1)} collective-permute-done((bf16[1,128,896]{2,1,0:T(8,128)(2,1)S(1)}, bf16[1,128,896]{2,1,0:T(8,128)(2,1)S(1)}, u32[]{:S(2)}, u32[]{:S(2)}) %collective-permute-start.5) | collective-permute-done | bytes 229408 | tf_op jit(solution)/shard_map/ppermute | solution.py:237
  87.9 1.0 %join.1 = bf16[1,128,3584]{2,1,0:T(8,128)(2,1)} custom-call(bf16[1,128,896]{2,1,0:T(8,128)(2,1)S(1)} %attend.3.a_ref, bf16[1,128,896]{2,1,0:T(8,128)(2,1)S(1)} %collective-permute-done.4.b_ref, bf16[1,128,896]{2,1,0:T(8,128)(2,1)S(1)} %collective-permute-done.5.c_ref, bf16[1,128,896]{2,1,0:T(8,128)(2,1)S(1)} %collective-permute-done.6.d_ref), custom_call_target="tpu_custom_call" | custom-call | tf_op jit(solution)/shard_map/join/pallas_call | solution.py:305
  (2 shorter events, 0.0 us)
Async XLA Ops:
  2.1 25.2 %all-to-all-start = ((bf16[64,32,128]{2,1,0:T(8,128)(2,1)}), bf16[64,32,128]{2,1,0:T(8,128)(2,1)S(1)}, u32[]{:S(2)}, u32[]{:S(2)}) async-start(bf16[64,32,128]{2,1,0:T(8,128)(2,1)} %prep_kv.1), calls=%async_computation | async-start | bytes 1048576 | tf_op jit(solution)/shard_map/all_to_all | solution.py:229
  27.3 32.5 %all-to-all-start.1 = ((bf16[32,120,128]{2,1,0:T(8,128)(2,1)}), bf16[32,120,128]{2,1,0:T(8,128)(2,1)}, u32[]{:S(2)}, u32[]{:S(2)}) async-start(bf16[32,120,128]{2,1,0:T(8,128)(2,1)} %prep_q.1), calls=%async_computation.1 | async-start | bytes 1966080 | tf_op jit(solution)/shard_map/all_to_all | solution.py:229
  32.4 14.6 %collective-permute-start.1 = (bf16[64,32,128]{2,1,0:T(8,128)(2,1)S(1)}, bf16[64,32,128]{2,1,0:T(8,128)(2,1)S(1)}, u32[]{:S(2)}, u32[]{:S(2)}) collective-permute-start(bf16[64,32,128]{2,1,0:T(8,128)(2,1)S(1)} %all-to-all-done.refs_0_), channel_id=1, source_target_pairs={{0,3},{1,0},{2,1},{3,2},{4,7},{5,4},{6,5},{7,6},{8,11},{9,8},{10,9... | collective-permute-start | bytes 1572872 | tf_op jit(solution)/shard_map/ppermute | solution.py:233
  35.5 15.3 %collective-permute-start = (bf16[64,32,128]{2,1,0:T(8,128)(2,1)S(1)}, bf16[64,32,128]{2,1,0:T(8,128)(2,1)S(1)}, u32[]{:S(2)}, u32[]{:S(2)}) collective-permute-start(bf16[64,32,128]{2,1,0:T(8,128)(2,1)S(1)} %all-to-all-done.refs_0_), channel_id=1, source_target_pairs={{0,1},{1,2},{2,3},{3,0},{4,5},{5,6},{6,7},{7,4},{8,9},{9,10},{10,1... | collective-permute-start | bytes 1572872 | tf_op jit(solution)/shard_map/ppermute | solution.py:233
  47.1 9.0 %collective-permute-start.3 = (bf16[64,16,128]{2,1,0:T(8,128)(2,1)S(1)}, bf16[64,16,128]{2,1,0:T(8,128)(2,1)S(1)}, u32[]{:S(2)}, u32[]{:S(2)}) collective-permute-start(bf16[64,16,128]{2,1,0:T(8,128)(2,1)S(1)} %slice.9), channel_id=1, source_target_pairs={{0,3},{1,0},{2,1},{3,2},{4,7},{5,4},{6,5},{7,6},{8,11},{9,8},{10,9... | collective-permute-start | bytes 786440 | tf_op jit(solution)/shard_map/ppermute | solution.py:233
  50.9 8.9 %copy-start = (s32[8]{0:T(128)S(1)}, s32[8]{0:T(128)}, u32[]{:S(2)}) copy-start(s32[8]{0:T(128)} %video_ref.5) | copy-start | bytes 100
  50.9 8.7 %collective-permute-start.2 = (bf16[64,16,128]{2,1,0:T(8,128)(2,1)S(1)}, bf16[64,16,128]{2,1,0:T(8,128)(2,1)S(1)}, u32[]{:S(2)}, u32[]{:S(2)}) collective-permute-start(bf16[64,16,128]{2,1,0:T(8,128)(2,1)S(1)} %slice.8), channel_id=1, source_target_pairs={{0,1},{1,2},{2,3},{3,0},{4,5},{5,6},{6,7},{7,4},{8,9},{9,10},{10,1... | collective-permute-start | bytes 786440 | tf_op jit(solution)/shard_map/ppermute | solution.py:233
  70.3 15.1 %collective-permute-start.4 = (bf16[1,128,896]{2,1,0:T(8,128)(2,1)S(1)}, bf16[1,128,896]{2,1,0:T(8,128)(2,1)S(1)}, u32[]{:S(2)}, u32[]{:S(2)}) collective-permute-start(bf16[1,128,896]{2,1,0:T(8,128)(2,1)S(1)} %get-tuple-element.11), channel_id=1, source_target_pairs={{0,4},{4,0},{8,12},{12,8},{1,5},{5,1},{9,13},{13,9},{2,6},{6,2},{1... | collective-permute-start | bytes 688136 | tf_op jit(solution)/shard_map/ppermute | solution.py:237
  71.1 14.3 %collective-permute-start.6 = (bf16[1,128,896]{2,1,0:T(8,128)(2,1)S(1)}, bf16[1,128,896]{2,1,0:T(8,128)(2,1)S(1)}, u32[]{:S(2)}, u32[]{:S(2)}) collective-permute-start(bf16[1,128,896]{2,1,0:T(8,128)(2,1)S(1)} %get-tuple-element.12), channel_id=1, source_target_pairs={{0,12},{4,8},{8,4},{12,0},{1,13},{5,9},{9,5},{13,1},{2,14},{6,10},... | collective-permute-start | bytes 688136 | tf_op jit(solution)/shard_map/ppermute | solution.py:237
  80.3 7.6 %collective-permute-start.5 = (bf16[1,128,896]{2,1,0:T(8,128)(2,1)S(1)}, bf16[1,128,896]{2,1,0:T(8,128)(2,1)S(1)}, u32[]{:S(2)}, u32[]{:S(2)}) collective-permute-start(bf16[1,128,896]{2,1,0:T(8,128)(2,1)S(1)} %attend.5), channel_id=1, source_target_pairs={{0,8},{4,12},{8,0},{12,4},{1,9},{5,13},{9,1},{13,5},{2,10},{6,14},... | collective-permute-start | bytes 688136 | tf_op jit(solution)/shard_map/ppermute | solution.py:237
